TPU v7x, 256 devices: a whole 4x4x8 slice. The times are simulated.
256 devices in a mesh: fsdp: 16 (over y, x_lo, core), replica: 16 (over z, x_hi).
Axes of the slice: x: 4 (x_hi: 2, x_lo: 2; x = x_hi * 2 + x_lo), y: 4, z: 8, core: 2. Of those that a mesh axis runs over, the one named last changes fastest.
Arguments:
- tokens: bfloat16 [16, 6144, 8192], P('replica', 'fsdp'), may hold values from -45 to 45
- key_grads: bfloat16 [16, 6144, 512], P('replica', 'fsdp'), may hold values from -45 to 45
- weights: float32 [16, 8192, 512], P('replica', 'fsdp'), may hold values from -6 to 6
- first_moment: float32 [16, 8192, 512], P('replica', 'fsdp'), may hold values from -4 to 4
- second_moment: float32 [16, 8192, 512], P('replica', 'fsdp'), may hold values from 0.01 to 1
- step_index: int32 [1], replicated, may hold values from 0 to 63
Outputs:
- new_weights: float32 [16, 8192, 512], P('replica', 'fsdp')
- new_first: float32 [16, 8192, 512], P('replica', 'fsdp')
- new_second: float32 [16, 8192, 512], P('replica', 'fsdp')
All inputs are finite; a program needn't handle non-finite values.
Results may differ from a plain program's by a relative error of at most 0.0005.
Values may be sent and summed in bfloat16 or wider, within the bound.
No kernel may reach another device: no remote copies, remote signals or barrier semaphores. Data moves between devices by JAX's collectives and lax.ppermute only.
A program may use at most 128 MiB of HBM per device.

v0:
```python
from functools import partial
import math

import jax
import jax.numpy as jnp
from jax import lax
from jax._src.lax.control_flow import conditionals
from jax.experimental import pallas as pl
from jax.experimental.pallas import tpu as pltpu
from jax.sharding import PartitionSpec as P


BETA_ONE = 0.9
BETA_TWO = 0.95
LEARN_RATE = 0.08
ADAM_EPS = 1e-08
NORM_EPS = 1e-06

SEND_SCALE = 2.0**-8
RAISE = 2.0**8

X, A, B = 1, 2, 4
PARTS = ((0, 176, (X, A, B)), (176, 176, (A, B, X)), (352, 160, (B, X, A)))


def neighbour(i, dim):
    y, x, c = i >> 2, (i >> 1) & 1, i & 1
    g = y ^ (y >> 1)
    if dim == X:
        x ^= 1
    elif dim == A:
        g ^= 1
    elif dim == B:
        g ^= 2
    else:
        c ^= 1
    y = g ^ (g >> 1)
    return (y << 2) | (x << 1) | c


def exchange(array, dim):
    return lax.ppermute(array, "fsdp", [(i, neighbour(i, dim)) for i in range(16)])


def from_partner(apart, array):
    return lax.ppermute(array, "replica", [(i, i ^ 1 << apart) for i in range(16)])


def block_of(me, d, flip):
    y, x, c = me >> 2, (me >> 1) & 1, me & 1
    g = (y ^ (y >> 1)) ^ (d >> 1)
    return ((g ^ (g >> 1)) << 2) | ((x ^ (d & 1)) << 1) | (c ^ flip)


CORNER = (7,)
FAR = (5, 3, 6)
NEAR = (1, 2, 4, 0)
PAIR = {X: (slice(0, 2), (5, 3)), A: (slice(1, 3), (3, 6)), B: (slice(0, 3, 2), (5, 6))}
VMEM_LIMIT = 24 << 20


def start_fetch(wanted, me, tokens, grads, outs, sems):
    copies = []
    for out, (order, flip) in zip(outs, wanted):
        for j, d in enumerate(order):
            column = pl.multiple_of(block_of(me[0], d, flip) * 512, 512)
            copies.append(
                pltpu.make_async_copy(
                    tokens.at[:, pl.ds(column, 512)],
                    out.at[:, pl.ds(j * 512, 512)],
                    sems.at[len(copies)],
                )
            )
        if out.shape[1] > 512 * len(order):
            copies.append(
                pltpu.make_async_copy(
                    grads, out.at[:, pl.ds(512 * len(order), 512)], sems.at[len(copies)]
                )
            )
    for copy in copies:
        copy.start()
    return copies


def fetch_kernel(wanted, me, tokens, grads, *refs):
    *outs, sems = refs
    for copy in start_fetch(wanted, me, tokens, grads, outs, sems):
        copy.wait()


def fetch(me, tokens, grads, wanted, widths):
    t = tokens.shape[0]
    return pl.pallas_call(
        partial(fetch_kernel, wanted),
        in_specs=[
            pl.BlockSpec(memory_space=pltpu.SMEM),
            pl.BlockSpec(memory_space=pltpu.HBM),
            pl.BlockSpec(memory_space=pltpu.HBM),
        ],
        out_shape=[pltpu.VMEM((t, width), tokens.dtype) for width in widths],
        scratch_shapes=[pltpu.SemaphoreType.DMA((8,))],
        cost_estimate=pl.CostEstimate(
            flops=0, bytes_accessed=4 * t * sum(widths), transcendentals=0
        ),
        compiler_params=pltpu.CompilerParams(vmem_limit_bytes=VMEM_LIMIT),
        name="fetch",
    )(
        me,
        pltpu.with_memory_space_constraint(tokens, pltpu.HBM),
        pltpu.with_memory_space_constraint(grads, pltpu.HBM),
    )


def hold_kernel(*refs):
    *pairs, sems = refs
    n = len(pairs) // 2
    copies = [pltpu.make_async_copy(pairs[i], pairs[n + i], sems.at[i]) for i in range(n)]
    for copy in copies:
        copy.start()
    for copy in copies:
        copy.wait()


def hold(*arrays):
    return pl.pallas_call(
        hold_kernel,
        in_specs=[pl.BlockSpec(memory_space=pltpu.HBM)] * len(arrays),
        out_shape=[pltpu.VMEM(a.shape, a.dtype) for a in arrays],
        scratch_shapes=[pltpu.SemaphoreType.DMA((len(arrays),))],
        compiler_params=pltpu.CompilerParams(vmem_limit_bytes=VMEM_LIMIT),
        name="hold",
    )(*[pltpu.with_memory_space_constraint(a, pltpu.HBM) for a in arrays])


def product_kernel(wanted, me, step_index, tokens, grads, mine, theirs, g_mine, g_theirs, *refs):
    out, level, *outs, both_tokens, both_grads, sems = refs
    t = g_mine.shape[0]
    copies = start_fetch(wanted, me, tokens, grads, outs, sems)
    level[0] = step_index[0] % 4
    both_grads[:t] = g_mine[:, 512:]
    both_grads[t:] = g_theirs[:, 512:]

    def block(j, _):
        column = pl.multiple_of(j * 512, 512)
        both_tokens[:t] = mine[:, pl.ds(column, 512)]
        both_tokens[t:] = theirs[:, pl.ds(column, 512)]
        out[j] = lax.dot_general(
            both_tokens[...],
            both_grads[...],
            (((0,), (0,)), ((), ())),
            preferred_element_type=jnp.float32,
        )
        return _

    lax.fori_loop(0, out.shape[0], block, None)
    for copy in copies:
        copy.wait()


def product(me, step_index, tokens, grads, mine, theirs, g_mine, g_theirs, blocks, wanted, widths):
    t, k = g_mine.shape[0], 512
    vmem = pl.BlockSpec(memory_space=pltpu.VMEM)
    smem = pl.BlockSpec(memory_space=pltpu.SMEM)
    hbm = pl.BlockSpec(memory_space=pltpu.HBM)
    return pl.pallas_call(
        partial(product_kernel, wanted),
        in_specs=[smem, smem, hbm, hbm] + [vmem] * 4,
        out_specs=[vmem, smem] + [vmem] * len(wanted),
        scratch_shapes=[
            pltpu.VMEM((2 * t, 512), mine.dtype),
            pltpu.VMEM((2 * t, k), mine.dtype),
            pltpu.SemaphoreType.DMA((8,)),
        ],
        out_shape=[
            pltpu.VMEM((blocks, 512, k), jnp.float32),
            jax.ShapeDtypeStruct((1,), jnp.int32),
        ]
        + [pltpu.VMEM((t, width), tokens.dtype) for width in widths],
        cost_estimate=pl.CostEstimate(
            flops=4 * t * 512 * blocks * k, bytes_accessed=4 * t * sum(widths), transcendentals=0
        ),
        compiler_params=pltpu.CompilerParams(vmem_limit_bytes=VMEM_LIMIT),
        name="product",
    )(
        me,
        step_index,
        pltpu.with_memory_space_constraint(tokens, pltpu.HBM),
        pltpu.with_memory_space_constraint(grads, pltpu.HBM),
        mine,
        theirs,
        g_mine,
        g_theirs,
    )


def squares_kernel(*refs):
    *pieces, out = refs
    total = sum(jnp.sum((p[...] * p[...]).reshape(-1, 8, 512), axis=0) for p in pieces)
    total = total[:, :128] + total[:, 128:256] + total[:, 256:384] + total[:, 384:]
    total = jnp.sum(total, axis=0, keepdims=True)
    out[...] = jnp.broadcast_to(total[None], out.shape)


def squares_of(pieces):
    return pl.pallas_call(
        squares_kernel,
        out_shape=jax.ShapeDtypeStruct((16, 1, 128), jnp.float32),
        compiler_params=pltpu.CompilerParams(vmem_limit_bytes=VMEM_LIMIT),
        name="squares",
    )(*pieces)


def adam_kernel(step_index, all_squares, *refs):
    *pieces, weights, first, second, updated, clip_out = refs
    squares = jnp.sum(all_squares[...], axis=0)
    squares = jnp.sum(squares, axis=1, keepdims=True)
    norm = jnp.sqrt(squares) * RAISE
    clip = jnp.minimum(1.0, math.sqrt(8192 * 512) / (norm + NORM_EPS)) * RAISE
    clip_out[...] = jnp.broadcast_to(clip, clip_out.shape)
    steps = jnp.full((1, 1), step_index[0] + 1, jnp.int32).astype(jnp.float32)
    rate = LEARN_RATE / (1.0 - jnp.exp(steps * math.log(BETA_ONE)))
    second_scale = 1.0 / (1.0 - jnp.exp(steps * math.log(BETA_TWO)))
    row = 0
    for piece in pieces:
        rows = pl.ds(row, piece.shape[0])
        row += piece.shape[0]
        clipped = clip * piece[...]
        one = BETA_ONE * first[rows] + (1.0 - BETA_ONE) * clipped
        two = BETA_TWO * second[rows] + (1.0 - BETA_TWO) * clipped * clipped
        updated[rows] = weights[rows] - rate * one / (jnp.sqrt(two * second_scale) + ADAM_EPS)


def adam(step_index, all_squares, pieces, weights, first, second):
    vmem = pl.BlockSpec(memory_space=pltpu.VMEM)
    return pl.pallas_call(
        adam_kernel,
        in_specs=[pl.BlockSpec(memory_space=pltpu.SMEM)] + [vmem] * (len(pieces) + 4),
        out_specs=[vmem] * 2,
        out_shape=[
            jax.ShapeDtypeStruct(weights.shape, jnp.float32),
            jax.ShapeDtypeStruct((8, 512), jnp.float32),
        ],
        compiler_params=pltpu.CompilerParams(vmem_limit_bytes=VMEM_LIMIT),
        name="adam",
    )(step_index, all_squares, *pieces, weights, first, second)


def moments_kernel(clip, *refs):
    *pieces, first, second, new_first, new_second = refs
    row = 0
    for piece in pieces:
        rows = pl.ds(row, piece.shape[0])
        row += piece.shape[0]
        clipped = clip[:1] * piece[...]
        new_first[rows] = BETA_ONE * first[rows] + (1.0 - BETA_ONE) * clipped
        new_second[rows] = BETA_TWO * second[rows] + (1.0 - BETA_TWO) * clipped * clipped


def moments(clip, pieces, first, second):
    vmem = pl.BlockSpec(memory_space=pltpu.VMEM)
    return pl.pallas_call(
        moments_kernel,
        in_specs=[vmem] * (len(pieces) + 3),
        out_specs=[vmem] * 2,
        out_shape=[jax.ShapeDtypeStruct(first.shape, jnp.float32)] * 2,
        cost_estimate=pl.CostEstimate(
            flops=8 * first.size, bytes_accessed=20 * first.size, transcendentals=0
        ),
        compiler_params=pltpu.CompilerParams(vmem_limit_bytes=VMEM_LIMIT),
        name="moments",
    )(clip, *pieces, first, second)


def finish(apart, packed, updated, clip, pieces, first, second):
    theirs = from_partner(apart, packed)
    new_first, new_second = moments(clip, pieces, first, second)
    new_weights = 0.5 * (updated + theirs.astype(jnp.float32))
    return new_weights, new_first, new_second


def local(tokens, key_grads, weights, first_moment, second_moment, step_index):
    inputs = tokens[0]
    grads_out = key_grads[0]
    me = lax.axis_index("fsdp")[None]

    source = (me, step_index, inputs, grads_out)
    (corner_out,) = fetch(me, inputs, grads_out, ((CORNER, 1),), (1024,))
    theirs_corner = exchange(corner_out, 0)
    far_out, mine_corner = fetch(
        me, inputs, grads_out, ((FAR, 1), (CORNER, 0)), (1536, 1024)
    )
    theirs_far = exchange(far_out, 0)
    grads_pair = (mine_corner, theirs_corner)
    acc_corner, _, mine_far = product(
        *source, mine_corner, theirs_corner, *grads_pair, 1, ((FAR, 0),), (1536,)
    )

    def own(d, row, rows):
        acc, slot = (acc_far, FAR.index(d)) if d in FAR else (acc_near, NEAR.index(d))
        return acc[slot, row : row + rows] * SEND_SCALE

    def pack(array):
        return array.astype(jnp.float16)

    parts = {dim: [p for at in range(3) for p in PARTS if p[2][at] == dim] for dim in (X, A, B)}
    packed = {}
    for dim in (X, A, B):
        row, rows, _ = parts[dim][0]
        packed[dim] = pack(acc_corner[0, row : row + rows] * SEND_SCALE)
    corner = {dim: exchange(packed[dim], dim) for dim in packed}
    mine_far, _ = lax.optimization_barrier((mine_far, packed))
    acc_far, level, near_out, mine_near = product(
        *source, mine_far, theirs_far, *grads_pair, 3, ((NEAR, 1), (NEAR, 0)), (2048, 2048)
    )
    theirs_near = exchange(near_out, 0)
    acc_near, _ = product(*source, mine_near, theirs_near, *grads_pair, 4, (), ())
    for dim in (X, A, B):
        row, rows, _ = parts[dim][0]
        packed[dim] = pack(acc_far[PAIR[dim][0], row : row + rows] * SEND_SCALE)
    pairs = {dim: exchange(packed[dim], dim) for dim in packed}

    def from_pair(dim, d):
        return pairs[dim][PAIR[dim][1].index(d)].astype(jnp.float32)

    for dim in (X, A, B):
        row, rows, (e1, e2, e3) = parts[dim][1]
        packed[dim] = pack(own(e2 | e3, row, rows) + corner[e1].astype(jnp.float32))
    ahead = {dim: exchange(packed[dim], dim) for dim in packed}
    for dim in (X, A, B):
        row, rows, _ = parts[dim][0]
        packed[dim] = pack(own(dim, row, rows))
    lasts = {dim: exchange(packed[dim], dim) for dim in packed}
    acc_near, _ = lax.optimization_barrier((acc_near, packed))
    for dim in (X, A, B):
        row, rows, (e1, e2, e3) = parts[dim][1]
        packed[dim] = pack(own(e2, row, rows) + from_pair(e1, e1 | e2))
    behinds = {dim: exchange(packed[dim], dim) for dim in packed}
    acc_near, _ = lax.optimization_barrier((acc_near, packed))
    for dim in (X, A, B):
        row, rows, (e1, e2, e3) = parts[dim][2]
        packed[dim] = pack(
            own(e3, row, rows) + from_pair(e1, e1 | e3) + ahead[e2].astype(jnp.float32)
        )
    thirds = {dim: exchange(packed[dim], dim) for dim in packed}
    acc_near, weights, first_moment, second_moment, _ = lax.optimization_barrier(
        (acc_near, weights[0], first_moment[0], second_moment[0], packed)
    )
    weights, first_moment, second_moment = hold(weights, first_moment, second_moment)
    acc_near, weights, first_moment, second_moment = lax.optimization_barrier(
        (acc_near, weights, first_moment, second_moment)
    )
    pieces = [
        own(0, row, rows)
        + lasts[e1].astype(jnp.float32)
        + behinds[e2].astype(jnp.float32)
        + thirds[e3].astype(jnp.float32)
        for row, rows, (e1, e2, e3) in PARTS
    ]

    all_squares = lax.all_to_all(squares_of(pieces), "fsdp", 0, 0, tiled=True)
    updated, clip = adam(step_index, all_squares, pieces, weights, first_moment, second_moment)
    outs = conditionals._switch_internal(
        level[0],
        [partial(finish, apart) for apart in range(4)],
        (pack(updated), updated, clip, pieces, first_moment, second_moment),
        branches_platforms=None,
    )
    return tuple(out[None] for out in outs)


def solution(mesh):
    spec = P("replica", "fsdp", None)
    return jax.shard_map(
        local,
        mesh=mesh,
        in_specs=(spec, spec, spec, spec, spec, P()),
        out_specs=(spec, spec, spec),
        check_vma=False,
    )
```

profile of v0, /device:TPU:1, one launch (start us, length us, event | category | flops | bytes accessed | tf_op | source)
XLA Modules:
  0.0 93.9 jit_solution(2000722109805887641)
XLA Ops:
  0.6 1.2 %fetch.3 = bf16[384,1024]{1,0:T(8,128)(2,1)S(1)} custom-call(s32[1]{0:T(128)} %bitcast.4.me, bf16[384,8192]{1,0:T(8,128)(2,1)} %bitcast.77, bf16[384,512]{1,0:T(8,128)(2,1)} %bitcast.82), custom_call_target="tpu_custom_call" | custom-call | bytes 1572864 | tf_op jit(solution)/shard_map/fetch/pallas_call | solution.py:93
  1.8 3.3 %collective-permute-start.4 = (bf16[384,1024]{1,0:T(8,128)(2,1)S(1)}, bf16[384,1024]{1,0:T(8,128)(2,1)S(1)}, u32[]{:S(2)}, u32[]{:S(2)}) collective-permute-start(bf16[384,1024]{1,0:T(8,128)(2,1)S(1)} %fetch.3), channel_id=1, source_target_pairs={{0,16},{16,0},{32,48},{48,32},{64,80},{80,64},{96,112},{112,96},{1... | collective-permute-start | bytes 2359304 | tf_op jit(solution)/shard_map/ppermute | solution.py:42
  5.1 1.6 %fetch.2 = (bf16[384,1536]{1,0:T(8,128)(2,1)S(1)}, bf16[384,1024]{1,0:T(8,128)(2,1)S(1)}) custom-call(s32[1]{0:T(128)} %bitcast.4.me, bf16[384,8192]{1,0:T(8,128)(2,1)} %bitcast.78, bf16[384,512]{1,0:T(8,128)(2,1)} %bitcast.83), custom_call_target="tpu_custom_call" | custom-call | bytes 3932160 | tf_op jit(solution)/shard_map/fetch/pallas_call | solution.py:93
  6.7 0.1 collective-permute-start.5
  7.5 0.0 collective-permute-done.4.theirs.g_theirs
  7.5 2.1 %product.3 = (f32[1,512,512]{2,1,0:T(8,128)S(1)}, s32[1]{0:T(128)}, bf16[384,1536]{1,0:T(8,128)(2,1)S(1)}) custom-call(s32[1]{0:T(128)} %bitcast.4.me, s32[1]{0:T(128)S(6)} %copy.21.step_index, bf16[384,8192]{1,0:T(8,128)(2,1)} %bitcast.79, bf16[384,512]{1,0:T(8,128)(2,1)} %bitcast.84, bf16[384,1024]{1,0:T(8,128)(2,1)S(1)} %get-tuple-element.136.mine.g_mine, ...), custom_call_target="tpu_custom_call" | custom-call | flops 402653184 | bytes 2359296 | tf_op jit(solution)/shard_map/product/pallas_call | solution.py:165
  9.6 0.1 fusion.13
  9.7 0.0 collective-permute-done.5.theirs
  9.7 2.5 %product.4 = (f32[3,512,512]{2,1,0:T(8,128)S(1)}, s32[1]{0:T(128)}, bf16[384,2048]{1,0:T(8,128)(2,1)S(1)}, bf16[384,2048]{1,0:T(8,128)(2,1)S(1)}) custom-call(s32[1]{0:T(128)} %bitcast.4.me, s32[1]{0:T(128)S(6)} %copy.21.step_index, bf16[384,8192]{1,0:T(8,128)(2,1)} %bitcast.80, bf16[384,512]{1,0:T(8,128)(2,1)} %bitcast.85, ...), custom_call_target="tpu_custom_call" | custom-call | flops 1207959552 | bytes 6291456 | tf_op jit(solution)/shard_map/product/pallas_call | solution.py:165
  12.2 0.6 collective-permute-start.6
  12.8 1.0 %collective-permute-start.12 = (f16[160,512]{1,0:T(8,128)(2,1)S(1)}, f16[160,512]{1,0:T(8,128)(2,1)S(1)}, u32[]{:S(2)}, u32[]{:S(2)}) collective-permute-start(f16[160,512]{1,0:T(8,128)(2,1)S(1)} %fusion.18), channel_id=1, source_target_pairs={{0,192},{16,208},{32,224},{48,240},{64,128},{80,144},{96,160},{112... | collective-permute-start | bytes 491528 | tf_op jit(solution)/shard_map/ppermute | solution.py:42
  13.8 1.2 %collective-permute-start.14 = (f16[176,512]{1,0:T(8,128)(2,1)S(1)}, f16[176,512]{1,0:T(8,128)(2,1)S(1)}, u32[]{:S(2)}, u32[]{:S(2)}) collective-permute-start(f16[176,512]{1,0:T(8,128)(2,1)S(1)} %get-tuple-element.177), channel_id=1, source_target_pairs={{0,32},{16,48},{32,0},{48,16},{64,96},{80,112},{96,64},{112,80},{1... | collective-permute-start | bytes 540680 | tf_op jit(solution)/shard_map/ppermute | solution.py:42
  15.0 4.6 %collective-permute-done.12 = f16[160,512]{1,0:T(8,128)(2,1)S(1)} collective-permute-done((f16[160,512]{1,0:T(8,128)(2,1)S(1)}, f16[160,512]{1,0:T(8,128)(2,1)S(1)}, u32[]{:S(2)}, u32[]{:S(2)}) %collective-permute-start.12) | collective-permute-done | bytes 163872 | tf_op jit(solution)/shard_map/ppermute | solution.py:42
  19.6 0.1 fusion.10
  19.7 0.1 collective-permute-start.13
  19.8 0.0 collective-permute-done.14
  19.8 0.1 fusion.6
  19.9 2.3 %collective-permute-start.11 = (f16[176,512]{1,0:T(8,128)(2,1)S(1)}, f16[176,512]{1,0:T(8,128)(2,1)S(1)}, u32[]{:S(2)}, u32[]{:S(2)}) collective-permute-start(f16[176,512]{1,0:T(8,128)(2,1)S(1)} %get-tuple-element.172), channel_id=1, source_target_pairs={{0,192},{16,208},{32,224},{48,240},{64,128},{80,144},{96,160},{112... | collective-permute-start | bytes 540680 | tf_op jit(solution)/shard_map/ppermute | solution.py:42
  22.2 0.1 multiply_convert_fusion.2
  22.3 0.6 collective-permute-start.7
  22.8 0.2 multiply_convert_fusion
  23.0 0.1 collective-permute-start.9
  23.1 0.0 collective-permute-done.6.theirs
  23.2 1.5 %collective-permute-start.8 = (f16[2,176,512]{2,1,0:T(8,128)(2,1)S(1)}, f16[2,176,512]{2,1,0:T(8,128)(2,1)S(1)}, u32[]{:S(2)}, u32[]{:S(2)}) collective-permute-start(f16[2,176,512]{2,1,0:T(8,128)(2,1)S(1)} %get-tuple-element.175), channel_id=1, source_target_pairs={{0,32},{16,48},{32,0},{48,16},{64,96},{80,112},{96,64},{112,80},{1... | collective-permute-start | bytes 1081352 | tf_op jit(solution)/shard_map/ppermute | solution.py:42
  24.7 2.7 %product.5 = (f32[4,512,512]{2,1,0:T(8,128)S(1)}, s32[1]{0:T(128)}) custom-call(s32[1]{0:T(128)} %bitcast.4.me, s32[1]{0:T(128)S(6)} %copy.21.step_index, bf16[384,8192]{1,0:T(8,128)(2,1)} %bitcast.81, bf16[384,512]{1,0:T(8,128)(2,1)} %bitcast.86, bf16[384,2048]{1,0:T(8,128)(2,1)S(1)} %get-tuple-element.142.mine, ...), custom_call_target="tpu_custom_call" | custom-call | flops 1610612736 | tf_op jit(solution)/shard_map/product/pallas_call | solution.py:165
  27.4 0.1 fusion.15
  27.5 5.9 %collective-permute-done.7 = f16[2,160,512]{2,1,0:T(8,128)(2,1)S(1)} collective-permute-done((f16[2,160,512]{2,1,0:T(8,128)(2,1)S(1)}, f16[2,160,512]{2,1,0:T(8,128)(2,1)S(1)}, u32[]{:S(2)}, u32[]{:S(2)}) %collective-permute-start.7) | collective-permute-done | bytes 327712 | tf_op jit(solution)/shard_map/ppermute | solution.py:42
  33.4 0.0 collective-permute-start.15
  33.4 0.1 fusion.20
  33.5 0.0 collective-permute-done.9
  33.5 2.0 %collective-permute-start.22 = (f16[160,512]{1,0:T(8,128)(2,1)S(1)}, f16[160,512]{1,0:T(8,128)(2,1)S(1)}, u32[]{:S(2)}, u32[]{:S(2)}) collective-permute-start(f16[160,512]{1,0:T(8,128)(2,1)S(1)} %fusion.19), channel_id=1, source_target_pairs={{0,192},{16,208},{32,224},{48,240},{64,128},{80,144},{96,160},{112... | collective-permute-start | bytes 491528 | tf_op jit(solution)/shard_map/ppermute | solution.py:42
  35.5 0.3 collective-permute-start.23
  35.8 0.1 fusion.17
  35.9 0.0 collective-permute-done.13
  35.9 0.9 %collective-permute-start.19 = (f16[176,512]{1,0:T(8,128)(2,1)S(1)}, f16[176,512]{1,0:T(8,128)(2,1)S(1)}, u32[]{:S(2)}, u32[]{:S(2)}) collective-permute-start(f16[176,512]{1,0:T(8,128)(2,1)S(1)} %get-tuple-element.170), channel_id=1, source_target_pairs={{0,64},{16,80},{32,96},{48,112},{64,0},{80,16},{96,32},{112,48},{1... | collective-permute-start | bytes 540680 | tf_op jit(solution)/shard_map/ppermute | solution.py:42
  36.9 0.1 fusion.11
  36.9 0.0 collective-permute-done.11
  36.9 1.3 %collective-permute-start.16 = (f16[176,512]{1,0:T(8,128)(2,1)S(1)}, f16[176,512]{1,0:T(8,128)(2,1)S(1)}, u32[]{:S(2)}, u32[]{:S(2)}) collective-permute-start(f16[176,512]{1,0:T(8,128)(2,1)S(1)} %get-tuple-element.171), channel_id=1, source_target_pairs={{0,32},{16,48},{32,0},{48,16},{64,96},{80,112},{96,64},{112,80},{1... | collective-permute-start | bytes 540680 | tf_op jit(solution)/shard_map/ppermute | solution.py:42
  38.2 0.0 collective-permute-done.15
  38.2 0.6 collective-permute-start.24
  38.8 0.2 fusion.7
  39.0 1.9 %hold.1 = (f32[512,512]{1,0:T(8,128)S(1)}, f32[512,512]{1,0:T(8,128)S(1)}, f32[512,512]{1,0:T(8,128)S(1)}) custom-call(f32[512,512]{1,0:T(8,128)} %bitcast.87, f32[512,512]{1,0:T(8,128)} %bitcast.88, f32[512,512]{1,0:T(8,128)} %bitcast.89), custom_call_target="tpu_custom_call" | custom-call | tf_op jit(solution)/shard_map/hold/pallas_call | solution.py:125
  40.9 0.5 collective-permute-start.21
  41.5 1.6 %collective-permute-start.18 = (f16[176,512]{1,0:T(8,128)(2,1)S(1)}, f16[176,512]{1,0:T(8,128)(2,1)S(1)}, u32[]{:S(2)}, u32[]{:S(2)}) collective-permute-start(f16[176,512]{1,0:T(8,128)(2,1)S(1)} %get-tuple-element.167), channel_id=1, source_target_pairs={{0,192},{16,208},{32,224},{48,240},{64,128},{80,144},{96,160},{112... | collective-permute-start | bytes 540680 | tf_op jit(solution)/shard_map/ppermute | solution.py:42
  43.1 2.9 %collective-permute-done.24 = f16[160,512]{1,0:T(8,128)(2,1)S(1)} collective-permute-done((f16[160,512]{1,0:T(8,128)(2,1)S(1)}, f16[160,512]{1,0:T(8,128)(2,1)S(1)}, u32[]{:S(2)}, u32[]{:S(2)}) %collective-permute-start.24) | collective-permute-done | bytes 163872 | tf_op jit(solution)/shard_map/ppermute | solution.py:42
  46.1 1.4 %collective-permute-start.20 = (f16[176,512]{1,0:T(8,128)(2,1)S(1)}, f16[176,512]{1,0:T(8,128)(2,1)S(1)}, u32[]{:S(2)}, u32[]{:S(2)}) collective-permute-start(f16[176,512]{1,0:T(8,128)(2,1)S(1)} %get-tuple-element.168), channel_id=1, source_target_pairs={{0,192},{16,208},{32,224},{48,240},{64,128},{80,144},{96,160},{112... | collective-permute-start | bytes 540680 | tf_op jit(solution)/shard_map/ppermute | solution.py:42
  47.5 0.0 collective-permute-done.19
  47.5 0.0 collective-permute-start.17
  47.5 0.1 fusion.9.refs_2_
  47.6 0.0 collective-permute-done.18
  47.6 5.2 %collective-permute-done.20 = f16[176,512]{1,0:T(8,128)(2,1)S(1)} collective-permute-done((f16[176,512]{1,0:T(8,128)(2,1)S(1)}, f16[176,512]{1,0:T(8,128)(2,1)S(1)}, u32[]{:S(2)}, u32[]{:S(2)}) %collective-permute-start.20) | collective-permute-done | bytes 180256 | tf_op jit(solution)/shard_map/ppermute | solution.py:42
  52.8 0.0 collective-permute-done.17
  52.8 0.2 fusion.1
  53.0 0.1 squares.1
  53.1 11.8 %all_to_all.5.all_squares = f32[16,1,128]{2,1,0:T(1,128)S(1)} all-to-all(f32[16,1,128]{2,1,0:T(1,128)S(1)} %squares.1), channel_id=1, replica_groups=mesh['fsdp'=16,'replica'=16] {'fsdp'}, dimensions={0} | all-to-all | bytes 16384 | tf_op jit(solution)/shard_map/all_to_all | solution.py:360
  64.9 1.2 %adam.1 = (f32[512,512]{1,0:T(8,128)S(1)}, f32[8,512]{1,0:T(8,128)S(1)}) custom-call(s32[1]{0:T(128)S(6)} %copy.21.step_index, f32[16,1,128]{2,1,0:T(1,128)S(1)} %all_to_all.5.all_squares, f32[176,512]{1,0:T(8,128)S(1)} %get-tuple-element.165.refs_0_, f32[176,512]{1,0:T(8,128)S(1)} %get-tuple-element.164.refs_1_, f32[160,512]{1,0:T(8,128)S(1)} %fusion.9.refs_2_, ...), custom_call_target="tpu_custom_call" | custom-call | tf_op jit(solution)/shard_map/adam/pallas_call | solution.py:235
  66.0 0.1 convert_element_type.213
  66.1 26.7 %conditional.1 = (f32[512,512]{1,0:T(8,128)}, f32[512,512]{1,0:T(8,128)}, f32[1,512,512]{2,1,0:T(8,128)S(1)}) conditional(s32[]{:T(128)} %bitcast.10, (f32[8,512]{1,0:T(8,128)S(1)}, f32[176,512]{1,0:T(8,128)S(1)}, f32[176,512]{1,0:T(8,128)S(1)}, f32[160,512]{1,0:T(8,128)S(1)}, f32[512,512]{1,0:T(8,128)S(1)}, ...), branch_computations={%region_0.0_spmd, %region_1.0_spmd, %region_2.0_spmd, %region_3.0_... | conditional | flops 2883584 | bytes 9961536 | solution.py:362
  66.8 3.1 %collective-permute-start.2 = (f16[512,512]{1,0:T(8,128)(2,1)S(1)}, f16[512,512]{1,0:T(8,128)(2,1)S(1)}, u32[]{:S(2)}, u32[]{:S(2)}) collective-permute-start(f16[512,512]{1,0:T(8,128)(2,1)S(1)} %get-tuple-element.94), channel_id=1, source_target_pairs={{0,4},{1,5},{2,6},{3,7},{4,0},{5,1},{6,2},{7,3},{8,12},{9,13},{10,... | collective-permute-start | bytes 1572872 | tf_op jit(solution)/shard_map/cond/branch_2_fun/ppermute | solution.py:46
  69.8 1.6 %moments.6 = (f32[512,512]{1,0:T(8,128)}, f32[512,512]{1,0:T(8,128)}) custom-call(f32[8,512]{1,0:T(8,128)S(1)} %get-tuple-element.85.clip, f32[176,512]{1,0:T(8,128)S(1)} %get-tuple-element.86.refs_0_, f32[176,512]{1,0:T(8,128)S(1)} %get-tuple-element.87.refs_1_, f32[160,512]{1,0:T(8,128)S(1)} %get-tuple-element.88.refs_2_, ...), custom_call_target="tpu_custom_call" | custom-call | flops 2097152 | bytes 5242880 | tf_op jit(solution)/shard_map/cond/branch_2_fun/moments/pallas_call | solution.py:261
  71.4 21.3 %collective-permute-done.2 = f16[512,512]{1,0:T(8,128)(2,1)S(1)} collective-permute-done((f16[512,512]{1,0:T(8,128)(2,1)S(1)}, f16[512,512]{1,0:T(8,128)(2,1)S(1)}, u32[]{:S(2)}, u32[]{:S(2)}) %collective-permute-start.2) | collective-permute-done | bytes 524320 | tf_op jit(solution)/shard_map/cond/branch_2_fun/ppermute | solution.py:46
  92.7 0.2 multiply_bitcast_fusion.2
  92.9 0.0 copy-start
  92.9 1.0 %copy-done = f32[1,512,512]{2,1,0:T(8,128)} copy-done((f32[1,512,512]{2,1,0:T(8,128)}, f32[1,512,512]{2,1,0:T(8,128)S(1)}, u32[]{:S(2)}) %copy-start) | copy-done | bytes 1048600
  (9 shorter events, 0.1 us)
Async XLA Ops:
  1.8 5.6 %collective-permute-start.4 = (bf16[384,1024]{1,0:T(8,128)(2,1)S(1)}, bf16[384,1024]{1,0:T(8,128)(2,1)S(1)}, u32[]{:S(2)}, u32[]{:S(2)}) collective-permute-start(bf16[384,1024]{1,0:T(8,128)(2,1)S(1)} %fetch.3), channel_id=1, source_target_pairs={{0,16},{16,0},{32,48},{48,32},{64,80},{80,64},{96,112},{112,96},{1... | collective-permute-start | bytes 2359304 | tf_op jit(solution)/shard_map/ppermute | solution.py:42
  6.7 3.0 %collective-permute-start.5 = (bf16[384,1536]{1,0:T(8,128)(2,1)S(1)}, bf16[384,1536]{1,0:T(8,128)(2,1)S(1)}, u32[]{:S(2)}, u32[]{:S(2)}) collective-permute-start(bf16[384,1536]{1,0:T(8,128)(2,1)S(1)} %get-tuple-element.140), channel_id=1, source_target_pairs={{0,16},{16,0},{32,48},{48,32},{64,80},{80,64},{96,112},{112,96},{1... | collective-permute-start | bytes 3538952 | tf_op jit(solution)/shard_map/ppermute | solution.py:42
  12.2 11.0 %collective-permute-start.6 = (bf16[384,2048]{1,0:T(8,128)(2,1)S(1)}, bf16[384,2048]{1,0:T(8,128)(2,1)S(1)}, u32[]{:S(2)}, u32[]{:S(2)}) collective-permute-start(bf16[384,2048]{1,0:T(8,128)(2,1)S(1)} %get-tuple-element.143), channel_id=1, source_target_pairs={{0,16},{16,0},{32,48},{48,32},{64,80},{80,64},{96,112},{112,96},{1... | collective-permute-start | bytes 4718600 | tf_op jit(solution)/shard_map/ppermute | solution.py:42
  12.8 6.9 %collective-permute-start.12 = (f16[160,512]{1,0:T(8,128)(2,1)S(1)}, f16[160,512]{1,0:T(8,128)(2,1)S(1)}, u32[]{:S(2)}, u32[]{:S(2)}) collective-permute-start(f16[160,512]{1,0:T(8,128)(2,1)S(1)} %fusion.18), channel_id=1, source_target_pairs={{0,192},{16,208},{32,224},{48,240},{64,128},{80,144},{96,160},{112... | collective-permute-start | bytes 491528 | tf_op jit(solution)/shard_map/ppermute | solution.py:42
  13.8 6.0 %collective-permute-start.10 = (f16[176,512]{1,0:T(8,128)(2,1)S(1)}, f16[176,512]{1,0:T(8,128)(2,1)S(1)}, u32[]{:S(2)}, u32[]{:S(2)}) collective-permute-start(f16[176,512]{1,0:T(8,128)(2,1)S(1)} %get-tuple-element.176), channel_id=1, source_target_pairs={{0,64},{16,80},{32,96},{48,112},{64,0},{80,16},{96,32},{112,48},{1... | collective-permute-start | bytes 540680 | tf_op jit(solution)/shard_map/ppermute | solution.py:42
  13.8 6.0 %collective-permute-start.14 = (f16[176,512]{1,0:T(8,128)(2,1)S(1)}, f16[176,512]{1,0:T(8,128)(2,1)S(1)}, u32[]{:S(2)}, u32[]{:S(2)}) collective-permute-start(f16[176,512]{1,0:T(8,128)(2,1)S(1)} %get-tuple-element.177), channel_id=1, source_target_pairs={{0,32},{16,48},{32,0},{48,16},{64,96},{80,112},{96,64},{112,80},{1... | collective-permute-start | bytes 540680 | tf_op jit(solution)/shard_map/ppermute | solution.py:42
  19.7 16.2 %collective-permute-start.13 = (f16[160,512]{1,0:T(8,128)(2,1)S(1)}, f16[160,512]{1,0:T(8,128)(2,1)S(1)}, u32[]{:S(2)}, u32[]{:S(2)}) collective-permute-start(f16[160,512]{1,0:T(8,128)(2,1)S(1)} %fusion.10), channel_id=1, source_target_pairs={{0,32},{16,48},{32,0},{48,16},{64,96},{80,112},{96,64},{112,80},{1... | collective-permute-start | bytes 491528 | tf_op jit(solution)/shard_map/ppermute | solution.py:42
  19.9 17.0 %collective-permute-start.11 = (f16[176,512]{1,0:T(8,128)(2,1)S(1)}, f16[176,512]{1,0:T(8,128)(2,1)S(1)}, u32[]{:S(2)}, u32[]{:S(2)}) collective-permute-start(f16[176,512]{1,0:T(8,128)(2,1)S(1)} %get-tuple-element.172), channel_id=1, source_target_pairs={{0,192},{16,208},{32,224},{48,240},{64,128},{80,144},{96,160},{112... | collective-permute-start | bytes 540680 | tf_op jit(solution)/shard_map/ppermute | solution.py:42
  22.3 11.1 %collective-permute-start.7 = (f16[2,160,512]{2,1,0:T(8,128)(2,1)S(1)}, f16[2,160,512]{2,1,0:T(8,128)(2,1)S(1)}, u32[]{:S(2)}, u32[]{:S(2)}) collective-permute-start(f16[2,160,512]{2,1,0:T(8,128)(2,1)S(1)} %multiply_convert_fusion.2), channel_id=1, source_target_pairs={{0,192},{16,208},{32,224},{48,240},{64,128},{80,144},{96,160},{112... | collective-permute-start | bytes 983048 | tf_op jit(solution)/shard_map/ppermute | solution.py:42
  23.0 10.4 %collective-permute-start.9 = (f16[2,176,512]{2,1,0:T(8,128)(2,1)S(1)}, f16[2,176,512]{2,1,0:T(8,128)(2,1)S(1)}, u32[]{:S(2)}, u32[]{:S(2)}) collective-permute-start(f16[2,176,512]{2,1,0:T(8,128)(2,1)S(1)} %get-tuple-element.174), channel_id=1, source_target_pairs={{0,64},{16,80},{32,96},{48,112},{64,0},{80,16},{96,32},{112,48},{1... | collective-permute-start | bytes 1081352 | tf_op jit(solution)/shard_map/ppermute | solution.py:42
  23.2 12.3 %collective-permute-start.8 = (f16[2,176,512]{2,1,0:T(8,128)(2,1)S(1)}, f16[2,176,512]{2,1,0:T(8,128)(2,1)S(1)}, u32[]{:S(2)}, u32[]{:S(2)}) collective-permute-start(f16[2,176,512]{2,1,0:T(8,128)(2,1)S(1)} %get-tuple-element.175), channel_id=1, source_target_pairs={{0,32},{16,48},{32,0},{48,16},{64,96},{80,112},{96,64},{112,80},{1... | collective-permute-start | bytes 1081352 | tf_op jit(solution)/shard_map/ppermute | solution.py:42
  33.4 4.8 %collective-permute-start.15 = (f16[176,512]{1,0:T(8,128)(2,1)S(1)}, f16[176,512]{1,0:T(8,128)(2,1)S(1)}, u32[]{:S(2)}, u32[]{:S(2)}) collective-permute-start(f16[176,512]{1,0:T(8,128)(2,1)S(1)} %get-tuple-element.173), channel_id=1, source_target_pairs={{0,64},{16,80},{32,96},{48,112},{64,0},{80,16},{96,32},{112,48},{1... | collective-permute-start | bytes 540680 | tf_op jit(solution)/shard_map/ppermute | solution.py:42
  33.5 7.5 %collective-permute-start.22 = (f16[160,512]{1,0:T(8,128)(2,1)S(1)}, f16[160,512]{1,0:T(8,128)(2,1)S(1)}, u32[]{:S(2)}, u32[]{:S(2)}) collective-permute-start(f16[160,512]{1,0:T(8,128)(2,1)S(1)} %fusion.19), channel_id=1, source_target_pairs={{0,192},{16,208},{32,224},{48,240},{64,128},{80,144},{96,160},{112... | collective-permute-start | bytes 491528 | tf_op jit(solution)/shard_map/ppermute | solution.py:42
  35.5 6.0 %collective-permute-start.23 = (f16[160,512]{1,0:T(8,128)(2,1)S(1)}, f16[160,512]{1,0:T(8,128)(2,1)S(1)}, u32[]{:S(2)}, u32[]{:S(2)}) collective-permute-start(f16[160,512]{1,0:T(8,128)(2,1)S(1)} %fusion.20), channel_id=1, source_target_pairs={{0,32},{16,48},{32,0},{48,16},{64,96},{80,112},{96,64},{112,80},{1... | collective-permute-start | bytes 491528 | tf_op jit(solution)/shard_map/ppermute | solution.py:42
  35.9 11.6 %collective-permute-start.19 = (f16[176,512]{1,0:T(8,128)(2,1)S(1)}, f16[176,512]{1,0:T(8,128)(2,1)S(1)}, u32[]{:S(2)}, u32[]{:S(2)}) collective-permute-start(f16[176,512]{1,0:T(8,128)(2,1)S(1)} %get-tuple-element.170), channel_id=1, source_target_pairs={{0,64},{16,80},{32,96},{48,112},{64,0},{80,16},{96,32},{112,48},{1... | collective-permute-start | bytes 540680 | tf_op jit(solution)/shard_map/ppermute | solution.py:42
  36.9 10.7 %collective-permute-start.16 = (f16[176,512]{1,0:T(8,128)(2,1)S(1)}, f16[176,512]{1,0:T(8,128)(2,1)S(1)}, u32[]{:S(2)}, u32[]{:S(2)}) collective-permute-start(f16[176,512]{1,0:T(8,128)(2,1)S(1)} %get-tuple-element.171), channel_id=1, source_target_pairs={{0,32},{16,48},{32,0},{48,16},{64,96},{80,112},{96,64},{112,80},{1... | collective-permute-start | bytes 540680 | tf_op jit(solution)/shard_map/ppermute | solution.py:42
  38.2 7.8 %collective-permute-start.24 = (f16[160,512]{1,0:T(8,128)(2,1)S(1)}, f16[160,512]{1,0:T(8,128)(2,1)S(1)}, u32[]{:S(2)}, u32[]{:S(2)}) collective-permute-start(f16[160,512]{1,0:T(8,128)(2,1)S(1)} %fusion.11), channel_id=1, source_target_pairs={{0,64},{16,80},{32,96},{48,112},{64,0},{80,16},{96,32},{112,48},{1... | collective-permute-start | bytes 491528 | tf_op jit(solution)/shard_map/ppermute | solution.py:42
  40.9 6.7 %collective-permute-start.21 = (f16[176,512]{1,0:T(8,128)(2,1)S(1)}, f16[176,512]{1,0:T(8,128)(2,1)S(1)}, u32[]{:S(2)}, u32[]{:S(2)}) collective-permute-start(f16[176,512]{1,0:T(8,128)(2,1)S(1)} %get-tuple-element.166), channel_id=1, source_target_pairs={{0,32},{16,48},{32,0},{48,16},{64,96},{80,112},{96,64},{112,80},{1... | collective-permute-start | bytes 540680 | tf_op jit(solution)/shard_map/ppermute | solution.py:42
  41.5 6.1 %collective-permute-start.18 = (f16[176,512]{1,0:T(8,128)(2,1)S(1)}, f16[176,512]{1,0:T(8,128)(2,1)S(1)}, u32[]{:S(2)}, u32[]{:S(2)}) collective-permute-start(f16[176,512]{1,0:T(8,128)(2,1)S(1)} %get-tuple-element.167), channel_id=1, source_target_pairs={{0,192},{16,208},{32,224},{48,240},{64,128},{80,144},{96,160},{112... | collective-permute-start | bytes 540680 | tf_op jit(solution)/shard_map/ppermute | solution.py:42
  46.1 6.7 %collective-permute-start.20 = (f16[176,512]{1,0:T(8,128)(2,1)S(1)}, f16[176,512]{1,0:T(8,128)(2,1)S(1)}, u32[]{:S(2)}, u32[]{:S(2)}) collective-permute-start(f16[176,512]{1,0:T(8,128)(2,1)S(1)} %get-tuple-element.168), channel_id=1, source_target_pairs={{0,192},{16,208},{32,224},{48,240},{64,128},{80,144},{96,160},{112... | collective-permute-start | bytes 540680 | tf_op jit(solution)/shard_map/ppermute | solution.py:42
  47.5 5.3 %collective-permute-start.17 = (f16[176,512]{1,0:T(8,128)(2,1)S(1)}, f16[176,512]{1,0:T(8,128)(2,1)S(1)}, u32[]{:S(2)}, u32[]{:S(2)}) collective-permute-start(f16[176,512]{1,0:T(8,128)(2,1)S(1)} %get-tuple-element.169), channel_id=1, source_target_pairs={{0,64},{16,80},{32,96},{48,112},{64,0},{80,16},{96,32},{112,48},{1... | collective-permute-start | bytes 540680 | tf_op jit(solution)/shard_map/ppermute | solution.py:42
  66.8 25.9 %collective-permute-start.2 = (f16[512,512]{1,0:T(8,128)(2,1)S(1)}, f16[512,512]{1,0:T(8,128)(2,1)S(1)}, u32[]{:S(2)}, u32[]{:S(2)}) collective-permute-start(f16[512,512]{1,0:T(8,128)(2,1)S(1)} %get-tuple-element.94), channel_id=1, source_target_pairs={{0,4},{1,5},{2,6},{3,7},{4,0},{5,1},{6,2},{7,3},{8,12},{9,13},{10,... | collective-permute-start | bytes 1572872 | tf_op jit(solution)/shard_map/cond/branch_2_fun/ppermute | solution.py:46
  92.9 1.0 %copy-start = (f32[1,512,512]{2,1,0:T(8,128)}, f32[1,512,512]{2,1,0:T(8,128)S(1)}, u32[]{:S(2)}) copy-start(f32[1,512,512]{2,1,0:T(8,128)S(1)} %get-tuple-element.133) | copy-start | bytes 3145732
where the time goes:
time: 94.1 us; the launch traced here: 93.9 us
  waiting for transfers between devices  40 us (43%)
  starting transfers between devices  22.5 us (24%)
  Pallas kernels  14.7 us (16%)
  blocking collectives  11.8 us (13%)
  other arithmetic  1.64 us (2%)
  between operations  1.56 us (2%)
  local copies, waits for them, and re-layouts  0.97 us (1%)
    ppermute x1, waiting for transfers between devices, from_partner(): lax.ppermute(array, 'replica', [(i, i ^ 1 << apart) for i in range(16)])  21.3 us
    ppermute x21, starting transfers between devices, exchange(): lax.ppermute(array, 'fsdp', [(i, neighbour(i, dim)) for i in range(16)])  19.5 us
    ppermute x21, waiting for transfers between devices, exchange(): lax.ppermute(array, 'fsdp', [(i, neighbour(i, dim)) for i in range(16)])  18.7 us
    all_to_all x1, blocking collectives, local(): all_squares = lax.all_to_all(squares_of(pieces), 'fsdp', 0, 0, tiled=True)  11.8 us
    pallas_call x3, Pallas kernels, product(): pl.pallas_call(partial(product_kernel, wanted), in_specs=[smem, smem, hbm...  7.27 us
    ppermute x1, starting transfers between devices, from_partner(): lax.ppermute(array, 'replica', [(i, i ^ 1 << apart) for i in range(16)])  3.06 us
    pallas_call x2, Pallas kernels, fetch(): pl.pallas_call(partial(fetch_kernel, wanted), in_specs=[pl.BlockSpec(memo...  2.75 us
    pallas_call x1, Pallas kernels, hold(): pl.pallas_call(hold_kernel, in_specs=[pl.BlockSpec(memory_space=pltpu.HBM...  1.89 us
  transfers between devices with their start and end apart: 22, of which 5 were waited for; matrix products, arithmetic and copies ran while one was open for 1% of the time, Pallas kernels for 10%

commit v1 on v0

--- a/solution.py
+++ b/solution.py
@@ -16,8 +16,7 @@
 ADAM_EPS = 1e-08
 NORM_EPS = 1e-06
 
-SEND_SCALE = 2.0**-8
-RAISE = 2.0**8
+FIRST_SCALE, SECOND_SCALE, THIRD_SCALE = 2.0**-5, 2.0**-6, 2.0**-7
 
 X, A, B = 1, 2, 4
 PARTS = ((0, 176, (X, A, B)), (176, 176, (A, B, X)), (352, 160, (B, X, A)))
@@ -111,8 +110,9 @@
     )
 
 
-def hold_kernel(*refs):
-    *pairs, sems = refs
+def hold_kernel(step_index, *refs):
+    *pairs, level, sems = refs
+    level[0] = step_index[0] % 4
     n = len(pairs) // 2
     copies = [pltpu.make_async_copy(pairs[i], pairs[n + i], sems.at[i]) for i in range(n)]
     for copy in copies:
@@ -121,22 +121,25 @@
         copy.wait()
 
 
-def hold(*arrays):
+def hold(step_index, *arrays):
     return pl.pallas_call(
         hold_kernel,
-        in_specs=[pl.BlockSpec(memory_space=pltpu.HBM)] * len(arrays),
-        out_shape=[pltpu.VMEM(a.shape, a.dtype) for a in arrays],
+        in_specs=[pl.BlockSpec(memory_space=pltpu.SMEM)]
+        + [pl.BlockSpec(memory_space=pltpu.HBM)] * len(arrays),
+        out_specs=[pl.BlockSpec(memory_space=pltpu.VMEM)] * len(arrays)
+        + [pl.BlockSpec(memory_space=pltpu.SMEM)],
+        out_shape=[pltpu.VMEM(a.shape, a.dtype) for a in arrays]
+        + [jax.ShapeDtypeStruct((1,), jnp.int32)],
         scratch_shapes=[pltpu.SemaphoreType.DMA((len(arrays),))],
         compiler_params=pltpu.CompilerParams(vmem_limit_bytes=VMEM_LIMIT),
         name="hold",
-    )(*[pltpu.with_memory_space_constraint(a, pltpu.HBM) for a in arrays])
-
-
-def product_kernel(wanted, me, step_index, tokens, grads, mine, theirs, g_mine, g_theirs, *refs):
-    out, level, *outs, both_tokens, both_grads, sems = refs
+    )(step_index, *[pltpu.with_memory_space_constraint(a, pltpu.HBM) for a in arrays])
+
+
+def product_kernel(wanted, me, tokens, grads, mine, theirs, g_mine, g_theirs, *refs):
+    out, *outs, both_tokens, both_grads, sems = refs
     t = g_mine.shape[0]
     copies = start_fetch(wanted, me, tokens, grads, outs, sems)
-    level[0] = step_index[0] % 4
     both_grads[:t] = g_mine[:, 512:]
     both_grads[t:] = g_theirs[:, 512:]
 
@@ -157,24 +160,21 @@
         copy.wait()
 
 
-def product(me, step_index, tokens, grads, mine, theirs, g_mine, g_theirs, blocks, wanted, widths):
+def product(me, tokens, grads, mine, theirs, g_mine, g_theirs, blocks, wanted, widths):
     t, k = g_mine.shape[0], 512
     vmem = pl.BlockSpec(memory_space=pltpu.VMEM)
     smem = pl.BlockSpec(memory_space=pltpu.SMEM)
     hbm = pl.BlockSpec(memory_space=pltpu.HBM)
     return pl.pallas_call(
         partial(product_kernel, wanted),
-        in_specs=[smem, smem, hbm, hbm] + [vmem] * 4,
-        out_specs=[vmem, smem] + [vmem] * len(wanted),
+        in_specs=[smem, hbm, hbm] + [vmem] * 4,
+        out_specs=[vmem] * (1 + len(wanted)),
         scratch_shapes=[
             pltpu.VMEM((2 * t, 512), mine.dtype),
             pltpu.VMEM((2 * t, k), mine.dtype),
             pltpu.SemaphoreType.DMA((8,)),
         ],
-        out_shape=[
-            pltpu.VMEM((blocks, 512, k), jnp.float32),
-            jax.ShapeDtypeStruct((1,), jnp.int32),
-        ]
+        out_shape=[pltpu.VMEM((blocks, 512, k), jnp.float32)]
         + [pltpu.VMEM((t, width), tokens.dtype) for width in widths],
         cost_estimate=pl.CostEstimate(
             flops=4 * t * 512 * blocks * k, bytes_accessed=4 * t * sum(widths), transcendentals=0
@@ -183,7 +183,6 @@
         name="product",
     )(
         me,
-        step_index,
         pltpu.with_memory_space_constraint(tokens, pltpu.HBM),
         pltpu.with_memory_space_constraint(grads, pltpu.HBM),
         mine,
@@ -214,8 +213,8 @@
     *pieces, weights, first, second, updated, clip_out = refs
     squares = jnp.sum(all_squares[...], axis=0)
     squares = jnp.sum(squares, axis=1, keepdims=True)
-    norm = jnp.sqrt(squares) * RAISE
-    clip = jnp.minimum(1.0, math.sqrt(8192 * 512) / (norm + NORM_EPS)) * RAISE
+    norm = jnp.sqrt(squares)
+    clip = jnp.minimum(1.0, math.sqrt(8192 * 512) / (norm + NORM_EPS))
     clip_out[...] = jnp.broadcast_to(clip, clip_out.shape)
     steps = jnp.full((1, 1), step_index[0] + 1, jnp.int32).astype(jnp.float32)
     rate = LEARN_RATE / (1.0 - jnp.exp(steps * math.log(BETA_ONE)))
@@ -283,7 +282,7 @@
     grads_out = key_grads[0]
     me = lax.axis_index("fsdp")[None]
 
-    source = (me, step_index, inputs, grads_out)
+    source = (me, inputs, grads_out)
     (corner_out,) = fetch(me, inputs, grads_out, ((CORNER, 1),), (1024,))
     theirs_corner = exchange(corner_out, 0)
     far_out, mine_corner = fetch(
@@ -291,69 +290,77 @@
     )
     theirs_far = exchange(far_out, 0)
     grads_pair = (mine_corner, theirs_corner)
-    acc_corner, _, mine_far = product(
+    acc_corner, mine_far = product(
         *source, mine_corner, theirs_corner, *grads_pair, 1, ((FAR, 0),), (1536,)
     )
 
     def own(d, row, rows):
         acc, slot = (acc_far, FAR.index(d)) if d in FAR else (acc_near, NEAR.index(d))
-        return acc[slot, row : row + rows] * SEND_SCALE
-
-    def pack(array):
-        return array.astype(jnp.float16)
+        return acc[slot, row : row + rows]
+
+    def pack(array, scale=1.0):
+        return (array * scale).astype(jnp.float16)
+
+    def unpack(message, scale):
+        return message.astype(jnp.float32) * (1.0 / scale)
 
     parts = {dim: [p for at in range(3) for p in PARTS if p[2][at] == dim] for dim in (X, A, B)}
     packed = {}
     for dim in (X, A, B):
         row, rows, _ = parts[dim][0]
-        packed[dim] = pack(acc_corner[0, row : row + rows] * SEND_SCALE)
+        packed[dim] = pack(acc_corner[0, row : row + rows], FIRST_SCALE)
     corner = {dim: exchange(packed[dim], dim) for dim in packed}
     mine_far, _ = lax.optimization_barrier((mine_far, packed))
-    acc_far, level, near_out, mine_near = product(
+    acc_far, near_out, mine_near = product(
         *source, mine_far, theirs_far, *grads_pair, 3, ((NEAR, 1), (NEAR, 0)), (2048, 2048)
     )
     theirs_near = exchange(near_out, 0)
-    acc_near, _ = product(*source, mine_near, theirs_near, *grads_pair, 4, (), ())
+    (acc_near,) = product(*source, mine_near, theirs_near, *grads_pair, 4, (), ())
     for dim in (X, A, B):
         row, rows, _ = parts[dim][0]
-        packed[dim] = pack(acc_far[PAIR[dim][0], row : row + rows] * SEND_SCALE)
+        packed[dim] = pack(acc_far[PAIR[dim][0], row : row + rows], FIRST_SCALE)
     pairs = {dim: exchange(packed[dim], dim) for dim in packed}
 
     def from_pair(dim, d):
-        return pairs[dim][PAIR[dim][1].index(d)].astype(jnp.float32)
+        return unpack(pairs[dim][PAIR[dim][1].index(d)], FIRST_SCALE)
 
     for dim in (X, A, B):
         row, rows, (e1, e2, e3) = parts[dim][1]
-        packed[dim] = pack(own(e2 | e3, row, rows) + corner[e1].astype(jnp.float32))
+        packed[dim] = pack(
+            own(e2 | e3, row, rows) + unpack(corner[e1], FIRST_SCALE), SECOND_SCALE
+        )
     ahead = {dim: exchange(packed[dim], dim) for dim in packed}
     for dim in (X, A, B):
         row, rows, _ = parts[dim][0]
-        packed[dim] = pack(own(dim, row, rows))
+        packed[dim] = pack(own(dim, row, rows), FIRST_SCALE)
     lasts = {dim: exchange(packed[dim], dim) for dim in packed}
     acc_near, _ = lax.optimization_barrier((acc_near, packed))
     for dim in (X, A, B):
         row, rows, (e1, e2, e3) = parts[dim][1]
-        packed[dim] = pack(own(e2, row, rows) + from_pair(e1, e1 | e2))
+        packed[dim] = pack(own(e2, row, rows) + from_pair(e1, e1 | e2), SECOND_SCALE)
     behinds = {dim: exchange(packed[dim], dim) for dim in packed}
     acc_near, _ = lax.optimization_barrier((acc_near, packed))
     for dim in (X, A, B):
         row, rows, (e1, e2, e3) = parts[dim][2]
         packed[dim] = pack(
-            own(e3, row, rows) + from_pair(e1, e1 | e3) + ahead[e2].astype(jnp.float32)
+            own(e3, row, rows) + from_pair(e1, e1 | e3) + unpack(ahead[e2], SECOND_SCALE),
+            THIRD_SCALE,
         )
     thirds = {dim: exchange(packed[dim], dim) for dim in packed}
     acc_near, weights, first_moment, second_moment, _ = lax.optimization_barrier(
         (acc_near, weights[0], first_moment[0], second_moment[0], packed)
     )
-    weights, first_moment, second_moment = hold(weights, first_moment, second_moment)
+    weights, first_moment, second_moment, level = hold(
+        step_index, weights, first_moment, second_moment
+    )
     acc_near, weights, first_moment, second_moment = lax.optimization_barrier(
         (acc_near, weights, first_moment, second_moment)
     )
     pieces = [
         own(0, row, rows)
-        + lasts[e1].astype(jnp.float32)
-        + behinds[e2].astype(jnp.float32)
-        + thirds[e3].astype(jnp.float32)
+        + unpack(lasts[e1], FIRST_SCALE)
+        + unpack(behinds[e2], SECOND_SCALE)
+        + unpack(thirds[e3], THIRD_SCALE)
         for row, rows, (e1, e2, e3) in PARTS
     ]
 

time: 94.1 us -> 91.3 us (0.970)
  waiting for transfers between devices: 40 us -> 35.8 us
  blocking collectives: 11.8 us -> 15.2 us
  starting transfers between devices: 22.5 us -> 20.9 us
    ppermute x21, waiting for transfers between devices: 18.7 us -> 14.6 us  [exchange(): lax.ppermute(array, 'fsdp', [(i, neighbour(i, dim)) for i in range(16)])]
    all_to_all x1, blocking collectives: 11.8 us -> 15.2 us  [local(): all_squares = lax.all_to_all(squares_of(pieces), 'fsdp', 0, 0, tiled=True)]
  transfers between devices with their start and end apart: 22 -> 22, of which waited for: 5 -> 11; matrix products, arithmetic and copies ran while one was open for 1% -> 1% of each run, Pallas kernels for 10% -> 11%
where the time goes in v1:
time: 91.3 us; the launch traced here: 91 us
  waiting for transfers between devices  35.8 us (39%)
  starting transfers between devices  20.9 us (23%)
  blocking collectives  15.2 us (17%)
  Pallas kernels  14.2 us (16%)
  other arithmetic  1.74 us (2%)
  between operations  1.51 us (2%)
  local copies, waits for them, and re-layouts  0.96 us (1%)
    ppermute x1, waiting for transfers between devices, from_partner(): lax.ppermute(array, 'replica', [(i, i ^ 1 << apart) for i in range(16)])  21.2 us
    ppermute x21, starting transfers between devices, exchange(): lax.ppermute(array, 'fsdp', [(i, neighbour(i, dim)) for i in range(16)])  18.6 us
    all_to_all x1, blocking collectives, local(): all_squares = lax.all_to_all(squares_of(pieces), 'fsdp', 0, 0, tiled=True)  15.2 us
    ppermute x21, waiting for transfers between devices, exchange(): lax.ppermute(array, 'fsdp', [(i, neighbour(i, dim)) for i in range(16)])  14.6 us
    pallas_call x3, Pallas kernels, product(): pl.pallas_call(partial(product_kernel, wanted), in_specs=[smem, hbm, hbm]...  6.25 us
    pallas_call x2, Pallas kernels, fetch(): pl.pallas_call(partial(fetch_kernel, wanted), in_specs=[pl.BlockSpec(memo...  2.75 us
    pallas_call x1, Pallas kernels, hold(): pl.pallas_call(hold_kernel, in_specs=[pl.BlockSpec(memory_space=pltpu.SME...  2.41 us
    ppermute x1, starting transfers between devices, from_partner(): lax.ppermute(array, 'replica', [(i, i ^ 1 << apart) for i in range(16)])  2.21 us
  transfers between devices with their start and end apart: 22, of which 11 were waited for; matrix products, arithmetic and copies ran while one was open for 1% of the time, Pallas kernels for 11%

profile of v1, /device:TPU:1, one launch (start us, length us, event | category | flops | bytes accessed | tf_op | source)
XLA Modules:
  0.0 91.0 jit_solution(3558020882599627985)
XLA Ops:
  0.6 1.2 %fetch.3 = bf16[384,1024]{1,0:T(8,128)(2,1)S(1)} custom-call(s32[1]{0:T(128)} %bitcast.4.me, bf16[384,8192]{1,0:T(8,128)(2,1)} %bitcast.89, bf16[384,512]{1,0:T(8,128)(2,1)} %bitcast.94), custom_call_target="tpu_custom_call" | custom-call | bytes 1572864 | tf_op jit(solution)/shard_map/fetch/pallas_call | solution.py:92
  1.8 3.3 %collective-permute-start.4 = (bf16[384,1024]{1,0:T(8,128)(2,1)S(1)}, bf16[384,1024]{1,0:T(8,128)(2,1)S(1)}, u32[]{:S(2)}, u32[]{:S(2)}) collective-permute-start(bf16[384,1024]{1,0:T(8,128)(2,1)S(1)} %fetch.3), channel_id=1, source_target_pairs={{0,16},{16,0},{32,48},{48,32},{64,80},{80,64},{96,112},{112,96},{1... | collective-permute-start | bytes 2359304 | tf_op jit(solution)/shard_map/ppermute | solution.py:41
  5.1 1.6 %fetch.2 = (bf16[384,1536]{1,0:T(8,128)(2,1)S(1)}, bf16[384,1024]{1,0:T(8,128)(2,1)S(1)}) custom-call(s32[1]{0:T(128)} %bitcast.4.me, bf16[384,8192]{1,0:T(8,128)(2,1)} %bitcast.90, bf16[384,512]{1,0:T(8,128)(2,1)} %bitcast.95), custom_call_target="tpu_custom_call" | custom-call | bytes 3932160 | tf_op jit(solution)/shard_map/fetch/pallas_call | solution.py:92
  6.7 0.1 collective-permute-start.5
  6.8 0.2 collective-permute-done.4.theirs.g_theirs
  7.0 1.6 %product.3 = (f32[1,512,512]{2,1,0:T(8,128)S(1)}, bf16[384,1536]{1,0:T(8,128)(2,1)S(1)}) custom-call(s32[1]{0:T(128)} %bitcast.4.me, bf16[384,8192]{1,0:T(8,128)(2,1)} %bitcast.91, bf16[384,512]{1,0:T(8,128)(2,1)} %bitcast.96, bf16[384,1024]{1,0:T(8,128)(2,1)S(1)} %get-tuple-element.135.mine.g_mine, ...), custom_call_target="tpu_custom_call" | custom-call | flops 402653184 | bytes 2359296 | tf_op jit(solution)/shard_map/product/pallas_call | solution.py:168
  8.7 0.1 fusion.22
  8.8 0.9 collective-permute-done.5.theirs
  9.6 2.0 %product.4 = (f32[3,512,512]{2,1,0:T(8,128)S(1)}, bf16[384,2048]{1,0:T(8,128)(2,1)S(1)}, bf16[384,2048]{1,0:T(8,128)(2,1)S(1)}) custom-call(s32[1]{0:T(128)} %bitcast.4.me, bf16[384,8192]{1,0:T(8,128)(2,1)} %bitcast.92, bf16[384,512]{1,0:T(8,128)(2,1)} %bitcast.97, bf16[384,1536]{1,0:T(8,128)(2,1)S(1)} %get-tuple-element.138.mine, ...), custom_call_target="tpu_custom_call" | custom-call | flops 1207959552 | bytes 6291456 | tf_op jit(solution)/shard_map/product/pallas_call | solution.py:168
  11.6 0.2 collective-permute-start.6
  11.8 1.0 %collective-permute-start.12 = (f16[160,512]{1,0:T(8,128)(2,1)S(1)}, f16[160,512]{1,0:T(8,128)(2,1)S(1)}, u32[]{:S(2)}, u32[]{:S(2)}) collective-permute-start(f16[160,512]{1,0:T(8,128)(2,1)S(1)} %fusion.27), channel_id=1, source_target_pairs={{0,192},{16,208},{32,224},{48,240},{64,128},{80,144},{96,160},{112... | collective-permute-start | bytes 491528 | tf_op jit(solution)/shard_map/ppermute | solution.py:41
  13.5 0.1 collective-permute-start.10
  13.6 1.3 %collective-permute-start.14 = (f16[176,512]{1,0:T(8,128)(2,1)S(1)}, f16[176,512]{1,0:T(8,128)(2,1)S(1)}, u32[]{:S(2)}, u32[]{:S(2)}) collective-permute-start(f16[176,512]{1,0:T(8,128)(2,1)S(1)} %get-tuple-element.175), channel_id=1, source_target_pairs={{0,32},{16,48},{32,0},{48,16},{64,96},{80,112},{96,64},{112,80},{1... | collective-permute-start | bytes 540680 | tf_op jit(solution)/shard_map/ppermute | solution.py:41
  14.9 3.5 %collective-permute-done.12 = f16[160,512]{1,0:T(8,128)(2,1)S(1)} collective-permute-done((f16[160,512]{1,0:T(8,128)(2,1)S(1)}, f16[160,512]{1,0:T(8,128)(2,1)S(1)}, u32[]{:S(2)}, u32[]{:S(2)}) %collective-permute-start.12) | collective-permute-done | bytes 163872 | tf_op jit(solution)/shard_map/ppermute | solution.py:41
  18.4 0.1 fusion.18
  18.5 0.1 collective-permute-start.13
  18.6 0.5 collective-permute-done.10
  19.1 0.1 collective-permute-done.14
  19.1 0.1 fusion.7
  19.3 1.2 %collective-permute-start.15 = (f16[176,512]{1,0:T(8,128)(2,1)S(1)}, f16[176,512]{1,0:T(8,128)(2,1)S(1)}, u32[]{:S(2)}, u32[]{:S(2)}) collective-permute-start(f16[176,512]{1,0:T(8,128)(2,1)S(1)} %get-tuple-element.170), channel_id=1, source_target_pairs={{0,64},{16,80},{32,96},{48,112},{64,0},{80,16},{96,32},{112,48},{1... | collective-permute-start | bytes 540680 | tf_op jit(solution)/shard_map/ppermute | solution.py:41
  20.5 0.1 multiply_convert_fusion.2
  20.5 1.7 %collective-permute-start.7 = (f16[2,160,512]{2,1,0:T(8,128)(2,1)S(1)}, f16[2,160,512]{2,1,0:T(8,128)(2,1)S(1)}, u32[]{:S(2)}, u32[]{:S(2)}) collective-permute-start(f16[2,160,512]{2,1,0:T(8,128)(2,1)S(1)} %multiply_convert_fusion.2), channel_id=1, source_target_pairs={{0,192},{16,208},{32,224},{48,240},{64,128},{80,144},{96,160},{112... | collective-permute-start | bytes 983048 | tf_op jit(solution)/shard_map/ppermute | solution.py:41
  22.3 0.2 multiply_convert_fusion
  22.5 0.1 collective-permute-start.9
  22.6 0.0 collective-permute-done.6.theirs
  22.6 0.4 collective-permute-start.8
  23.0 2.7 %product.5 = f32[4,512,512]{2,1,0:T(8,128)S(1)} custom-call(s32[1]{0:T(128)} %bitcast.4.me, bf16[384,8192]{1,0:T(8,128)(2,1)} %bitcast.93, bf16[384,512]{1,0:T(8,128)(2,1)} %bitcast.98, bf16[384,2048]{1,0:T(8,128)(2,1)S(1)} %get-tuple-element.140.mine, bf16[384,2048]{1,0:T(8,128)(2,1)S(1)} %collective-permute-done.6.theirs, ...), custom_call_target="tpu_custom_call" | custom-call | flops 1610612736 | tf_op jit(solution)/shard_map/product/pallas_call | solution.py:168
  25.6 0.1 fusion.26
  25.7 2.0 %collective-permute-done.7 = f16[2,160,512]{2,1,0:T(8,128)(2,1)S(1)} collective-permute-done((f16[2,160,512]{2,1,0:T(8,128)(2,1)S(1)}, f16[2,160,512]{2,1,0:T(8,128)(2,1)S(1)}, u32[]{:S(2)}, u32[]{:S(2)}) %collective-permute-start.7) | collective-permute-done | bytes 327712 | tf_op jit(solution)/shard_map/ppermute | solution.py:41
  27.8 1.6 %collective-permute-start.11 = (f16[176,512]{1,0:T(8,128)(2,1)S(1)}, f16[176,512]{1,0:T(8,128)(2,1)S(1)}, u32[]{:S(2)}, u32[]{:S(2)}) collective-permute-start(f16[176,512]{1,0:T(8,128)(2,1)S(1)} %get-tuple-element.171), channel_id=1, source_target_pairs={{0,192},{16,208},{32,224},{48,240},{64,128},{80,144},{96,160},{112... | collective-permute-start | bytes 540680 | tf_op jit(solution)/shard_map/ppermute | solution.py:41
  29.4 0.1 fusion.28
  29.5 2.8 %collective-permute-done.9 = f16[2,176,512]{2,1,0:T(8,128)(2,1)S(1)} collective-permute-done((f16[2,176,512]{2,1,0:T(8,128)(2,1)S(1)}, f16[2,176,512]{2,1,0:T(8,128)(2,1)S(1)}, u32[]{:S(2)}, u32[]{:S(2)}) %collective-permute-start.9) | collective-permute-done | bytes 360480 | tf_op jit(solution)/shard_map/ppermute | solution.py:41
  32.3 1.3 %collective-permute-start.22 = (f16[160,512]{1,0:T(8,128)(2,1)S(1)}, f16[160,512]{1,0:T(8,128)(2,1)S(1)}, u32[]{:S(2)}, u32[]{:S(2)}) collective-permute-start(f16[160,512]{1,0:T(8,128)(2,1)S(1)} %fusion.29), channel_id=1, source_target_pairs={{0,192},{16,208},{32,224},{48,240},{64,128},{80,144},{96,160},{112... | collective-permute-start | bytes 491528 | tf_op jit(solution)/shard_map/ppermute | solution.py:41
  33.6 0.0 collective-permute-done.8
  33.6 0.1 fusion.24
  33.7 0.0 collective-permute-done.13
  33.7 0.9 collective-permute-start.19
  34.7 0.1 fusion.20
  34.7 0.0 collective-permute-done.15
  34.8 0.7 collective-permute-start.16
  35.5 0.0 collective-permute-done.11
  35.5 1.4 %collective-permute-start.24 = (f16[160,512]{1,0:T(8,128)(2,1)S(1)}, f16[160,512]{1,0:T(8,128)(2,1)S(1)}, u32[]{:S(2)}, u32[]{:S(2)}) collective-permute-start(f16[160,512]{1,0:T(8,128)(2,1)S(1)} %fusion.20), channel_id=1, source_target_pairs={{0,64},{16,80},{32,96},{48,112},{64,0},{80,16},{96,32},{112,48},{1... | collective-permute-start | bytes 491528 | tf_op jit(solution)/shard_map/ppermute | solution.py:41
  37.0 0.2 fusion.9
  37.2 2.4 %hold.1 = (f32[512,512]{1,0:T(8,128)S(1)}, f32[512,512]{1,0:T(8,128)S(1)}, f32[512,512]{1,0:T(8,128)S(1)}, s32[1]{0:T(128)}) custom-call(s32[1]{0:T(128)S(6)} %copy.21.step_index, f32[512,512]{1,0:T(8,128)} %bitcast.99, f32[512,512]{1,0:T(8,128)} %bitcast.100, f32[512,512]{1,0:T(8,128)} %bitcast.101), custom_call_target="tpu_custom_call" | custom-call | tf_op jit(solution)/shard_map/hold/pallas_call | solution.py:125
  39.6 0.0 collective-permute-done.22
  39.6 1.7 %collective-permute-start.18 = (f16[176,512]{1,0:T(8,128)(2,1)S(1)}, f16[176,512]{1,0:T(8,128)(2,1)S(1)}, u32[]{:S(2)}, u32[]{:S(2)}) collective-permute-start(f16[176,512]{1,0:T(8,128)(2,1)S(1)} %get-tuple-element.164), channel_id=1, source_target_pairs={{0,192},{16,208},{32,224},{48,240},{64,128},{80,144},{96,160},{112... | collective-permute-start | bytes 540680 | tf_op jit(solution)/shard_map/ppermute | solution.py:41
  41.3 0.2 collective-permute-start.21
  41.5 1.2 %collective-permute-start.20 = (f16[176,512]{1,0:T(8,128)(2,1)S(1)}, f16[176,512]{1,0:T(8,128)(2,1)S(1)}, u32[]{:S(2)}, u32[]{:S(2)}) collective-permute-start(f16[176,512]{1,0:T(8,128)(2,1)S(1)} %get-tuple-element.166), channel_id=1, source_target_pairs={{0,192},{16,208},{32,224},{48,240},{64,128},{80,144},{96,160},{112... | collective-permute-start | bytes 540680 | tf_op jit(solution)/shard_map/ppermute | solution.py:41
  42.7 0.1 fusion.16.refs_2_
  42.8 2.6 %collective-permute-done.18 = f16[176,512]{1,0:T(8,128)(2,1)S(1)} collective-permute-done((f16[176,512]{1,0:T(8,128)(2,1)S(1)}, f16[176,512]{1,0:T(8,128)(2,1)S(1)}, u32[]{:S(2)}, u32[]{:S(2)}) %collective-permute-start.18) | collective-permute-done | bytes 180256 | tf_op jit(solution)/shard_map/ppermute | solution.py:41
  45.4 0.2 collective-permute-done.21
  45.6 1.7 %collective-permute-done.20 = f16[176,512]{1,0:T(8,128)(2,1)S(1)} collective-permute-done((f16[176,512]{1,0:T(8,128)(2,1)S(1)}, f16[176,512]{1,0:T(8,128)(2,1)S(1)}, u32[]{:S(2)}, u32[]{:S(2)}) %collective-permute-start.20) | collective-permute-done | bytes 180256 | tf_op jit(solution)/shard_map/ppermute | solution.py:41
  47.4 0.2 fusion.3
  47.6 0.1 squares.1
  47.7 15.2 %all_to_all.5.all_squares = f32[16,1,128]{2,1,0:T(1,128)S(1)} all-to-all(f32[16,1,128]{2,1,0:T(1,128)S(1)} %squares.1), channel_id=1, replica_groups=mesh['fsdp'=16,'replica'=16] {'fsdp'}, dimensions={0} | all-to-all | bytes 16384 | tf_op jit(solution)/shard_map/all_to_all | solution.py:367
  62.9 1.2 %adam.1 = (f32[512,512]{1,0:T(8,128)S(1)}, f32[8,512]{1,0:T(8,128)S(1)}) custom-call(s32[1]{0:T(128)S(6)} %copy.21.step_index, f32[16,1,128]{2,1,0:T(1,128)S(1)} %all_to_all.5.all_squares, f32[176,512]{1,0:T(8,128)S(1)} %get-tuple-element.163.refs_0_, f32[176,512]{1,0:T(8,128)S(1)} %get-tuple-element.162.refs_1_, f32[160,512]{1,0:T(8,128)S(1)} %fusion.16.refs_2_, ...), custom_call_target="tpu_custom_call" | custom-call | tf_op jit(solution)/shard_map/adam/pallas_call | solution.py:234
  64.1 0.1 convert_element_type.192
  64.2 25.9 %conditional.1 = (f32[512,512]{1,0:T(8,128)}, f32[512,512]{1,0:T(8,128)}, f32[1,512,512]{2,1,0:T(8,128)S(1)}) conditional(s32[]{:T(128)} %bitcast.25, (f32[8,512]{1,0:T(8,128)S(1)}, f32[176,512]{1,0:T(8,128)S(1)}, f32[176,512]{1,0:T(8,128)S(1)}, f32[160,512]{1,0:T(8,128)S(1)}, f32[512,512]{1,0:T(8,128)S(1)}, ...), branch_computations={%region_0.0_spmd, %region_1.0_spmd, %region_2.0_spmd, %region_3.0_... | conditional | flops 2883584 | bytes 9961536 | solution.py:369
  64.8 2.2 %collective-permute-start.2 = (f16[512,512]{1,0:T(8,128)(2,1)S(1)}, f16[512,512]{1,0:T(8,128)(2,1)S(1)}, u32[]{:S(2)}, u32[]{:S(2)}) collective-permute-start(f16[512,512]{1,0:T(8,128)(2,1)S(1)} %get-tuple-element.94), channel_id=1, source_target_pairs={{0,4},{1,5},{2,6},{3,7},{4,0},{5,1},{6,2},{7,3},{8,12},{9,13},{10,... | collective-permute-start | bytes 1572872 | tf_op jit(solution)/shard_map/cond/branch_2_fun/ppermute | solution.py:45
  67.1 1.6 %moments.6 = (f32[512,512]{1,0:T(8,128)}, f32[512,512]{1,0:T(8,128)}) custom-call(f32[8,512]{1,0:T(8,128)S(1)} %get-tuple-element.85.clip, f32[176,512]{1,0:T(8,128)S(1)} %get-tuple-element.86.refs_0_, f32[176,512]{1,0:T(8,128)S(1)} %get-tuple-element.87.refs_1_, f32[160,512]{1,0:T(8,128)S(1)} %get-tuple-element.88.refs_2_, ...), custom_call_target="tpu_custom_call" | custom-call | flops 2097152 | bytes 5242880 | tf_op jit(solution)/shard_map/cond/branch_2_fun/moments/pallas_call | solution.py:260
  68.6 21.2 %collective-permute-done.2 = f16[512,512]{1,0:T(8,128)(2,1)S(1)} collective-permute-done((f16[512,512]{1,0:T(8,128)(2,1)S(1)}, f16[512,512]{1,0:T(8,128)(2,1)S(1)}, u32[]{:S(2)}, u32[]{:S(2)}) %collective-permute-start.2) | collective-permute-done | bytes 524320 | tf_op jit(solution)/shard_map/cond/branch_2_fun/ppermute | solution.py:45
  89.9 0.2 multiply_bitcast_fusion.2
  90.1 0.0 copy-start
  90.1 1.0 %copy-done = f32[1,512,512]{2,1,0:T(8,128)} copy-done((f32[1,512,512]{2,1,0:T(8,128)}, f32[1,512,512]{2,1,0:T(8,128)S(1)}, u32[]{:S(2)}) %copy-start) | copy-done | bytes 1048600
  (9 shorter events, 0.1 us)
Async XLA Ops:
  1.8 5.2 %collective-permute-start.4 = (bf16[384,1024]{1,0:T(8,128)(2,1)S(1)}, bf16[384,1024]{1,0:T(8,128)(2,1)S(1)}, u32[]{:S(2)}, u32[]{:S(2)}) collective-permute-start(bf16[384,1024]{1,0:T(8,128)(2,1)S(1)} %fetch.3), channel_id=1, source_target_pairs={{0,16},{16,0},{32,48},{48,32},{64,80},{80,64},{96,112},{112,96},{1... | collective-permute-start | bytes 2359304 | tf_op jit(solution)/shard_map/ppermute | solution.py:41
  6.7 2.9 %collective-permute-start.5 = (bf16[384,1536]{1,0:T(8,128)(2,1)S(1)}, bf16[384,1536]{1,0:T(8,128)(2,1)S(1)}, u32[]{:S(2)}, u32[]{:S(2)}) collective-permute-start(bf16[384,1536]{1,0:T(8,128)(2,1)S(1)} %get-tuple-element.139), channel_id=1, source_target_pairs={{0,16},{16,0},{32,48},{48,32},{64,80},{80,64},{96,112},{112,96},{1... | collective-permute-start | bytes 3538952 | tf_op jit(solution)/shard_map/ppermute | solution.py:41
  11.6 11.0 %collective-permute-start.6 = (bf16[384,2048]{1,0:T(8,128)(2,1)S(1)}, bf16[384,2048]{1,0:T(8,128)(2,1)S(1)}, u32[]{:S(2)}, u32[]{:S(2)}) collective-permute-start(bf16[384,2048]{1,0:T(8,128)(2,1)S(1)} %get-tuple-element.141), channel_id=1, source_target_pairs={{0,16},{16,0},{32,48},{48,32},{64,80},{80,64},{96,112},{112,96},{1... | collective-permute-start | bytes 4718600 | tf_op jit(solution)/shard_map/ppermute | solution.py:41
  11.8 6.6 %collective-permute-start.12 = (f16[160,512]{1,0:T(8,128)(2,1)S(1)}, f16[160,512]{1,0:T(8,128)(2,1)S(1)}, u32[]{:S(2)}, u32[]{:S(2)}) collective-permute-start(f16[160,512]{1,0:T(8,128)(2,1)S(1)} %fusion.27), channel_id=1, source_target_pairs={{0,192},{16,208},{32,224},{48,240},{64,128},{80,144},{96,160},{112... | collective-permute-start | bytes 491528 | tf_op jit(solution)/shard_map/ppermute | solution.py:41
  13.5 5.5 %collective-permute-start.10 = (f16[176,512]{1,0:T(8,128)(2,1)S(1)}, f16[176,512]{1,0:T(8,128)(2,1)S(1)}, u32[]{:S(2)}, u32[]{:S(2)}) collective-permute-start(f16[176,512]{1,0:T(8,128)(2,1)S(1)} %get-tuple-element.174), channel_id=1, source_target_pairs={{0,64},{16,80},{32,96},{48,112},{64,0},{80,16},{96,32},{112,48},{1... | collective-permute-start | bytes 540680 | tf_op jit(solution)/shard_map/ppermute | solution.py:41
  13.6 5.5 %collective-permute-start.14 = (f16[176,512]{1,0:T(8,128)(2,1)S(1)}, f16[176,512]{1,0:T(8,128)(2,1)S(1)}, u32[]{:S(2)}, u32[]{:S(2)}) collective-permute-start(f16[176,512]{1,0:T(8,128)(2,1)S(1)} %get-tuple-element.175), channel_id=1, source_target_pairs={{0,32},{16,48},{32,0},{48,16},{64,96},{80,112},{96,64},{112,80},{1... | collective-permute-start | bytes 540680 | tf_op jit(solution)/shard_map/ppermute | solution.py:41
  18.5 15.2 %collective-permute-start.13 = (f16[160,512]{1,0:T(8,128)(2,1)S(1)}, f16[160,512]{1,0:T(8,128)(2,1)S(1)}, u32[]{:S(2)}, u32[]{:S(2)}) collective-permute-start(f16[160,512]{1,0:T(8,128)(2,1)S(1)} %fusion.18), channel_id=1, source_target_pairs={{0,32},{16,48},{32,0},{48,16},{64,96},{80,112},{96,64},{112,80},{1... | collective-permute-start | bytes 491528 | tf_op jit(solution)/shard_map/ppermute | solution.py:41
  19.3 15.5 %collective-permute-start.15 = (f16[176,512]{1,0:T(8,128)(2,1)S(1)}, f16[176,512]{1,0:T(8,128)(2,1)S(1)}, u32[]{:S(2)}, u32[]{:S(2)}) collective-permute-start(f16[176,512]{1,0:T(8,128)(2,1)S(1)} %get-tuple-element.170), channel_id=1, source_target_pairs={{0,64},{16,80},{32,96},{48,112},{64,0},{80,16},{96,32},{112,48},{1... | collective-permute-start | bytes 540680 | tf_op jit(solution)/shard_map/ppermute | solution.py:41
  20.5 7.2 %collective-permute-start.7 = (f16[2,160,512]{2,1,0:T(8,128)(2,1)S(1)}, f16[2,160,512]{2,1,0:T(8,128)(2,1)S(1)}, u32[]{:S(2)}, u32[]{:S(2)}) collective-permute-start(f16[2,160,512]{2,1,0:T(8,128)(2,1)S(1)} %multiply_convert_fusion.2), channel_id=1, source_target_pairs={{0,192},{16,208},{32,224},{48,240},{64,128},{80,144},{96,160},{112... | collective-permute-start | bytes 983048 | tf_op jit(solution)/shard_map/ppermute | solution.py:41
  22.5 9.8 %collective-permute-start.9 = (f16[2,176,512]{2,1,0:T(8,128)(2,1)S(1)}, f16[2,176,512]{2,1,0:T(8,128)(2,1)S(1)}, u32[]{:S(2)}, u32[]{:S(2)}) collective-permute-start(f16[2,176,512]{2,1,0:T(8,128)(2,1)S(1)} %get-tuple-element.172), channel_id=1, source_target_pairs={{0,64},{16,80},{32,96},{48,112},{64,0},{80,16},{96,32},{112,48},{1... | collective-permute-start | bytes 1081352 | tf_op jit(solution)/shard_map/ppermute | solution.py:41
  22.6 11.0 %collective-permute-start.8 = (f16[2,176,512]{2,1,0:T(8,128)(2,1)S(1)}, f16[2,176,512]{2,1,0:T(8,128)(2,1)S(1)}, u32[]{:S(2)}, u32[]{:S(2)}) collective-permute-start(f16[2,176,512]{2,1,0:T(8,128)(2,1)S(1)} %get-tuple-element.173), channel_id=1, source_target_pairs={{0,32},{16,48},{32,0},{48,16},{64,96},{80,112},{96,64},{112,80},{1... | collective-permute-start | bytes 1081352 | tf_op jit(solution)/shard_map/ppermute | solution.py:41
  27.8 7.7 %collective-permute-start.11 = (f16[176,512]{1,0:T(8,128)(2,1)S(1)}, f16[176,512]{1,0:T(8,128)(2,1)S(1)}, u32[]{:S(2)}, u32[]{:S(2)}) collective-permute-start(f16[176,512]{1,0:T(8,128)(2,1)S(1)} %get-tuple-element.171), channel_id=1, source_target_pairs={{0,192},{16,208},{32,224},{48,240},{64,128},{80,144},{96,160},{112... | collective-permute-start | bytes 540680 | tf_op jit(solution)/shard_map/ppermute | solution.py:41
  32.3 7.3 %collective-permute-start.22 = (f16[160,512]{1,0:T(8,128)(2,1)S(1)}, f16[160,512]{1,0:T(8,128)(2,1)S(1)}, u32[]{:S(2)}, u32[]{:S(2)}) collective-permute-start(f16[160,512]{1,0:T(8,128)(2,1)S(1)} %fusion.29), channel_id=1, source_target_pairs={{0,192},{16,208},{32,224},{48,240},{64,128},{80,144},{96,160},{112... | collective-permute-start | bytes 491528 | tf_op jit(solution)/shard_map/ppermute | solution.py:41
  33.6 7.7 %collective-permute-start.23 = (f16[160,512]{1,0:T(8,128)(2,1)S(1)}, f16[160,512]{1,0:T(8,128)(2,1)S(1)}, u32[]{:S(2)}, u32[]{:S(2)}) collective-permute-start(f16[160,512]{1,0:T(8,128)(2,1)S(1)} %fusion.28), channel_id=1, source_target_pairs={{0,32},{16,48},{32,0},{48,16},{64,96},{80,112},{96,64},{112,80},{1... | collective-permute-start | bytes 491528 | tf_op jit(solution)/shard_map/ppermute | solution.py:41
  33.7 8.9 %collective-permute-start.19 = (f16[176,512]{1,0:T(8,128)(2,1)S(1)}, f16[176,512]{1,0:T(8,128)(2,1)S(1)}, u32[]{:S(2)}, u32[]{:S(2)}) collective-permute-start(f16[176,512]{1,0:T(8,128)(2,1)S(1)} %get-tuple-element.168), channel_id=1, source_target_pairs={{0,64},{16,80},{32,96},{48,112},{64,0},{80,16},{96,32},{112,48},{1... | collective-permute-start | bytes 540680 | tf_op jit(solution)/shard_map/ppermute | solution.py:41
  34.8 8.0 %collective-permute-start.16 = (f16[176,512]{1,0:T(8,128)(2,1)S(1)}, f16[176,512]{1,0:T(8,128)(2,1)S(1)}, u32[]{:S(2)}, u32[]{:S(2)}) collective-permute-start(f16[176,512]{1,0:T(8,128)(2,1)S(1)} %get-tuple-element.169), channel_id=1, source_target_pairs={{0,32},{16,48},{32,0},{48,16},{64,96},{80,112},{96,64},{112,80},{1... | collective-permute-start | bytes 540680 | tf_op jit(solution)/shard_map/ppermute | solution.py:41
  35.5 6.0 %collective-permute-start.24 = (f16[160,512]{1,0:T(8,128)(2,1)S(1)}, f16[160,512]{1,0:T(8,128)(2,1)S(1)}, u32[]{:S(2)}, u32[]{:S(2)}) collective-permute-start(f16[160,512]{1,0:T(8,128)(2,1)S(1)} %fusion.20), channel_id=1, source_target_pairs={{0,64},{16,80},{32,96},{48,112},{64,0},{80,16},{96,32},{112,48},{1... | collective-permute-start | bytes 491528 | tf_op jit(solution)/shard_map/ppermute | solution.py:41
  39.6 5.8 %collective-permute-start.18 = (f16[176,512]{1,0:T(8,128)(2,1)S(1)}, f16[176,512]{1,0:T(8,128)(2,1)S(1)}, u32[]{:S(2)}, u32[]{:S(2)}) collective-permute-start(f16[176,512]{1,0:T(8,128)(2,1)S(1)} %get-tuple-element.164), channel_id=1, source_target_pairs={{0,192},{16,208},{32,224},{48,240},{64,128},{80,144},{96,160},{112... | collective-permute-start | bytes 540680 | tf_op jit(solution)/shard_map/ppermute | solution.py:41
  41.3 4.3 %collective-permute-start.21 = (f16[176,512]{1,0:T(8,128)(2,1)S(1)}, f16[176,512]{1,0:T(8,128)(2,1)S(1)}, u32[]{:S(2)}, u32[]{:S(2)}) collective-permute-start(f16[176,512]{1,0:T(8,128)(2,1)S(1)} %get-tuple-element.165), channel_id=1, source_target_pairs={{0,32},{16,48},{32,0},{48,16},{64,96},{80,112},{96,64},{112,80},{1... | collective-permute-start | bytes 540680 | tf_op jit(solution)/shard_map/ppermute | solution.py:41
  41.5 5.9 %collective-permute-start.20 = (f16[176,512]{1,0:T(8,128)(2,1)S(1)}, f16[176,512]{1,0:T(8,128)(2,1)S(1)}, u32[]{:S(2)}, u32[]{:S(2)}) collective-permute-start(f16[176,512]{1,0:T(8,128)(2,1)S(1)} %get-tuple-element.166), channel_id=1, source_target_pairs={{0,192},{16,208},{32,224},{48,240},{64,128},{80,144},{96,160},{112... | collective-permute-start | bytes 540680 | tf_op jit(solution)/shard_map/ppermute | solution.py:41
  42.7 4.7 %collective-permute-start.17 = (f16[176,512]{1,0:T(8,128)(2,1)S(1)}, f16[176,512]{1,0:T(8,128)(2,1)S(1)}, u32[]{:S(2)}, u32[]{:S(2)}) collective-permute-start(f16[176,512]{1,0:T(8,128)(2,1)S(1)} %get-tuple-element.167), channel_id=1, source_target_pairs={{0,64},{16,80},{32,96},{48,112},{64,0},{80,16},{96,32},{112,48},{1... | collective-permute-start | bytes 540680 | tf_op jit(solution)/shard_map/ppermute | solution.py:41
  64.8 25.0 %collective-permute-start.2 = (f16[512,512]{1,0:T(8,128)(2,1)S(1)}, f16[512,512]{1,0:T(8,128)(2,1)S(1)}, u32[]{:S(2)}, u32[]{:S(2)}) collective-permute-start(f16[512,512]{1,0:T(8,128)(2,1)S(1)} %get-tuple-element.94), channel_id=1, source_target_pairs={{0,4},{1,5},{2,6},{3,7},{4,0},{5,1},{6,2},{7,3},{8,12},{9,13},{10,... | collective-permute-start | bytes 1572872 | tf_op jit(solution)/shard_map/cond/branch_2_fun/ppermute | solution.py:45
  90.1 1.0 %copy-start = (f32[1,512,512]{2,1,0:T(8,128)}, f32[1,512,512]{2,1,0:T(8,128)S(1)}, u32[]{:S(2)}) copy-start(f32[1,512,512]{2,1,0:T(8,128)S(1)} %get-tuple-element.132) | copy-start | bytes 3145732

commit v2 on v1

--- a/solution.py
+++ b/solution.py
@@ -209,7 +209,7 @@
     )(*pieces)
 
 
-def adam_kernel(step_index, all_squares, *refs):
+def adam_kernel(start, step_index, all_squares, *refs):
     *pieces, weights, first, second, updated, clip_out = refs
     squares = jnp.sum(all_squares[...], axis=0)
     squares = jnp.sum(squares, axis=1, keepdims=True)
@@ -219,26 +219,30 @@
     steps = jnp.full((1, 1), step_index[0] + 1, jnp.int32).astype(jnp.float32)
     rate = LEARN_RATE / (1.0 - jnp.exp(steps * math.log(BETA_ONE)))
     second_scale = 1.0 / (1.0 - jnp.exp(steps * math.log(BETA_TWO)))
-    row = 0
+    row = start
     for piece in pieces:
         rows = pl.ds(row, piece.shape[0])
+        mine = pl.ds(row - start, piece.shape[0])
         row += piece.shape[0]
         clipped = clip * piece[...]
         one = BETA_ONE * first[rows] + (1.0 - BETA_ONE) * clipped
         two = BETA_TWO * second[rows] + (1.0 - BETA_TWO) * clipped * clipped
-        updated[rows] = weights[rows] - rate * one / (jnp.sqrt(two * second_scale) + ADAM_EPS)
-
-
-def adam(step_index, all_squares, pieces, weights, first, second):
+        updated[mine] = weights[rows] - rate * one / (jnp.sqrt(two * second_scale) + ADAM_EPS)
+
+
+def adam(start, step_index, all_squares, pieces, weights, first, second):
     vmem = pl.BlockSpec(memory_space=pltpu.VMEM)
     return pl.pallas_call(
-        adam_kernel,
+        partial(adam_kernel, start),
         in_specs=[pl.BlockSpec(memory_space=pltpu.SMEM)] + [vmem] * (len(pieces) + 4),
         out_specs=[vmem] * 2,
         out_shape=[
-            jax.ShapeDtypeStruct(weights.shape, jnp.float32),
+            jax.ShapeDtypeStruct((sum(p.shape[0] for p in pieces), 512), jnp.float32),
             jax.ShapeDtypeStruct((8, 512), jnp.float32),
         ],
+        cost_estimate=pl.CostEstimate(
+            flops=20 * 512 * 512, bytes_accessed=16 * 512 * 512, transcendentals=512 * 512
+        ),
         compiler_params=pltpu.CompilerParams(vmem_limit_bytes=VMEM_LIMIT),
         name="adam",
     )(step_index, all_squares, *pieces, weights, first, second)
@@ -270,10 +274,16 @@
     )(clip, *pieces, first, second)
 
 
-def finish(apart, packed, updated, clip, pieces, first, second):
+def finish(apart, packed, updated, clip, pieces, weights, first, second, step_index, all_squares):
+    f32 = jnp.float32
     theirs = from_partner(apart, packed)
+    start = packed.shape[0]
+    behind, _ = adam(start, step_index, all_squares, pieces[1:], weights, first, second)
+    theirs_behind = from_partner(apart, behind.astype(jnp.float16))
     new_first, new_second = moments(clip, pieces, first, second)
-    new_weights = 0.5 * (updated + theirs.astype(jnp.float32))
+    new_weights = jnp.concatenate(
+        [0.5 * (updated + theirs.astype(f32)), 0.5 * (behind + theirs_behind.astype(f32))]
+    )
     return new_weights, new_first, new_second
 
 
@@ -285,14 +295,12 @@
     source = (me, inputs, grads_out)
     (corner_out,) = fetch(me, inputs, grads_out, ((CORNER, 1),), (1024,))
     theirs_corner = exchange(corner_out, 0)
-    far_out, mine_corner = fetch(
-        me, inputs, grads_out, ((FAR, 1), (CORNER, 0)), (1536, 1024)
+    far_out, mine_corner, mine_far = fetch(
+        me, inputs, grads_out, ((FAR, 1), (CORNER, 0), (FAR, 0)), (1536, 1024, 1536)
     )
     theirs_far = exchange(far_out, 0)
     grads_pair = (mine_corner, theirs_corner)
-    acc_corner, mine_far = product(
-        *source, mine_corner, theirs_corner, *grads_pair, 1, ((FAR, 0),), (1536,)
-    )
+    (acc_corner,) = product(*source, mine_corner, theirs_corner, *grads_pair, 1, (), ())
 
     def own(d, row, rows):
         acc, slot = (acc_far, FAR.index(d)) if d in FAR else (acc_near, NEAR.index(d))
@@ -365,11 +373,23 @@
     ]
 
     all_squares = lax.all_to_all(squares_of(pieces), "fsdp", 0, 0, tiled=True)
-    updated, clip = adam(step_index, all_squares, pieces, weights, first_moment, second_moment)
+    updated, clip = adam(
+        0, step_index, all_squares, pieces[:1], weights, first_moment, second_moment
+    )
     outs = conditionals._switch_internal(
         level[0],
         [partial(finish, apart) for apart in range(4)],
-        (pack(updated), updated, clip, pieces, first_moment, second_moment),
+        (
+            pack(updated),
+            updated,
+            clip,
+            pieces,
+            weights,
+            first_moment,
+            second_moment,
+            step_index,
+            all_squares,
+        ),
         branches_platforms=None,
     )
     return tuple(out[None] for out in outs)

time: 91.3 us -> 90.8 us (level)
  waiting for transfers between devices: 35.8 us -> 34.6 us
    ppermute x1 -> x2, waiting for transfers between devices: 21.2 us -> 19 us  [from_partner(): lax.ppermute(array, 'replica', [(i, i ^ 1 << apart) for i in range(16)])]
    pallas_call x1 -> x2, Pallas kernels: 1.16 us -> 2.21 us  [adam(): pl.pallas_call(partial(adam_kernel, start), in_specs=[pl.BlockSpec(memory...]
    ppermute x21, waiting for transfers between devices: 14.6 us -> 15.6 us  [exchange(): lax.ppermute(array, 'fsdp', [(i, neighbour(i, dim)) for i in range(16)])]
    pallas_call x3, Pallas kernels: 6.25 us -> 5.33 us  [product(): pl.pallas_call(partial(product_kernel, wanted), in_specs=[smem, hbm, hbm]...]
    ppermute x1 -> x2, starting transfers between devices: 2.21 us -> 2.54 us  [from_partner(): lax.ppermute(array, 'replica', [(i, i ^ 1 << apart) for i in range(16)])]
  transfers between devices with their start and end apart: 22 -> 23, of which waited for: 11 -> 11; matrix products, arithmetic and copies ran while one was open for 1% -> 2% of each run, Pallas kernels for 11% -> 12%
where the time goes in v2:
time: 90.8 us; the launch traced here: 90.6 us
  waiting for transfers between devices  34.6 us (38%)
  starting transfers between devices  21.1 us (23%)
  blocking collectives  15.2 us (17%)
  Pallas kernels  14.7 us (16%)
  other arithmetic  1.79 us (2%)
  between operations  1.51 us (2%)
  local copies, waits for them, and re-layouts  0.96 us (1%)
    ppermute x2, waiting for transfers between devices, from_partner(): lax.ppermute(array, 'replica', [(i, i ^ 1 << apart) for i in range(16)])  19 us
    ppermute x21, starting transfers between devices, exchange(): lax.ppermute(array, 'fsdp', [(i, neighbour(i, dim)) for i in range(16)])  18.6 us
    ppermute x21, waiting for transfers between devices, exchange(): lax.ppermute(array, 'fsdp', [(i, neighbour(i, dim)) for i in range(16)])  15.6 us
    all_to_all x1, blocking collectives, local(): all_squares = lax.all_to_all(squares_of(pieces), 'fsdp', 0, 0, tiled=True)  15.2 us
    pallas_call x3, Pallas kernels, product(): pl.pallas_call(partial(product_kernel, wanted), in_specs=[smem, hbm, hbm]...  5.33 us
    pallas_call x2, Pallas kernels, fetch(): pl.pallas_call(partial(fetch_kernel, wanted), in_specs=[pl.BlockSpec(memo...  3.11 us
    ppermute x2, starting transfers between devices, from_partner(): lax.ppermute(array, 'replica', [(i, i ^ 1 << apart) for i in range(16)])  2.54 us
    pallas_call x1, Pallas kernels, hold(): pl.pallas_call(hold_kernel, in_specs=[pl.BlockSpec(memory_space=pltpu.SME...  2.41 us
  transfers between devices with their start and end apart: 23, of which 11 were waited for; matrix products, arithmetic and copies ran while one was open for 2% of the time, Pallas kernels for 12%

profile of v2, /device:TPU:1, one launch (start us, length us, event | category | flops | bytes accessed | tf_op | source)
XLA Modules:
  0.0 90.6 jit_solution(9419012371143201623)
XLA Ops:
  0.6 1.2 %fetch.3 = bf16[384,1024]{1,0:T(8,128)(2,1)S(1)} custom-call(s32[1]{0:T(128)} %bitcast.4.me, bf16[384,8192]{1,0:T(8,128)(2,1)} %bitcast.89, bf16[384,512]{1,0:T(8,128)(2,1)} %bitcast.94), custom_call_target="tpu_custom_call" | custom-call | bytes 1572864 | tf_op jit(solution)/shard_map/fetch/pallas_call | solution.py:92
  1.8 3.3 %collective-permute-start.8 = (bf16[384,1024]{1,0:T(8,128)(2,1)S(1)}, bf16[384,1024]{1,0:T(8,128)(2,1)S(1)}, u32[]{:S(2)}, u32[]{:S(2)}) collective-permute-start(bf16[384,1024]{1,0:T(8,128)(2,1)S(1)} %fetch.3), channel_id=1, source_target_pairs={{0,16},{16,0},{32,48},{48,32},{64,80},{80,64},{96,112},{112,96},{1... | collective-permute-start | bytes 2359304 | tf_op jit(solution)/shard_map/ppermute | solution.py:41
  5.1 1.9 %fetch.2 = (bf16[384,1536]{1,0:T(8,128)(2,1)S(1)}, bf16[384,1024]{1,0:T(8,128)(2,1)S(1)}, bf16[384,1536]{1,0:T(8,128)(2,1)S(1)}) custom-call(s32[1]{0:T(128)} %bitcast.4.me, bf16[384,8192]{1,0:T(8,128)(2,1)} %bitcast.90, bf16[384,512]{1,0:T(8,128)(2,1)} %bitcast.95), custom_call_target="tpu_custom_call" | custom-call | bytes 6291456 | tf_op jit(solution)/shard_map/fetch/pallas_call | solution.py:92
  7.0 0.1 collective-permute-start.9
  7.2 0.0 collective-permute-done.8.theirs.g_theirs
  7.2 0.7 product.3
  7.9 0.1 fusion.27
  8.0 2.0 %collective-permute-done.9.theirs = bf16[384,1536]{1,0:T(8,128)(2,1)S(1)} collective-permute-done((bf16[384,1536]{1,0:T(8,128)(2,1)S(1)}, bf16[384,1536]{1,0:T(8,128)(2,1)S(1)}, u32[]{:S(2)}, u32[]{:S(2)}) %collective-permute-start.9) | collective-permute-done | bytes 1179680 | tf_op jit(solution)/shard_map/ppermute | solution.py:41
  10.0 2.0 %product.4 = (f32[3,512,512]{2,1,0:T(8,128)S(1)}, bf16[384,2048]{1,0:T(8,128)(2,1)S(1)}, bf16[384,2048]{1,0:T(8,128)(2,1)S(1)}) custom-call(s32[1]{0:T(128)} %bitcast.4.me, bf16[384,8192]{1,0:T(8,128)(2,1)} %bitcast.92, bf16[384,512]{1,0:T(8,128)(2,1)} %bitcast.97, bf16[384,1536]{1,0:T(8,128)(2,1)S(1)} %get-tuple-element.176.mine, ...), custom_call_target="tpu_custom_call" | custom-call | flops 1207959552 | bytes 6291456 | tf_op jit(solution)/shard_map/product/pallas_call | solution.py:168
  12.0 0.2 collective-permute-start.10
  12.2 1.0 %collective-permute-start.16 = (f16[160,512]{1,0:T(8,128)(2,1)S(1)}, f16[160,512]{1,0:T(8,128)(2,1)S(1)}, u32[]{:S(2)}, u32[]{:S(2)}) collective-permute-start(f16[160,512]{1,0:T(8,128)(2,1)S(1)} %fusion.31), channel_id=1, source_target_pairs={{0,192},{16,208},{32,224},{48,240},{64,128},{80,144},{96,160},{112... | collective-permute-start | bytes 491528 | tf_op jit(solution)/shard_map/ppermute | solution.py:41
  13.9 0.1 collective-permute-start.14
  14.0 1.3 %collective-permute-start.18 = (f16[176,512]{1,0:T(8,128)(2,1)S(1)}, f16[176,512]{1,0:T(8,128)(2,1)S(1)}, u32[]{:S(2)}, u32[]{:S(2)}) collective-permute-start(f16[176,512]{1,0:T(8,128)(2,1)S(1)} %get-tuple-element.213), channel_id=1, source_target_pairs={{0,32},{16,48},{32,0},{48,16},{64,96},{80,112},{96,64},{112,80},{1... | collective-permute-start | bytes 540680 | tf_op jit(solution)/shard_map/ppermute | solution.py:41
  15.3 3.5 %collective-permute-done.16 = f16[160,512]{1,0:T(8,128)(2,1)S(1)} collective-permute-done((f16[160,512]{1,0:T(8,128)(2,1)S(1)}, f16[160,512]{1,0:T(8,128)(2,1)S(1)}, u32[]{:S(2)}, u32[]{:S(2)}) %collective-permute-start.16) | collective-permute-done | bytes 163872 | tf_op jit(solution)/shard_map/ppermute | solution.py:41
  18.8 0.1 fusion.21
  18.9 0.1 collective-permute-start.17
  19.0 0.5 collective-permute-done.14
  19.4 0.1 collective-permute-done.18
  19.5 0.1 fusion.9
  19.7 1.2 %collective-permute-start.19 = (f16[176,512]{1,0:T(8,128)(2,1)S(1)}, f16[176,512]{1,0:T(8,128)(2,1)S(1)}, u32[]{:S(2)}, u32[]{:S(2)}) collective-permute-start(f16[176,512]{1,0:T(8,128)(2,1)S(1)} %get-tuple-element.208), channel_id=1, source_target_pairs={{0,64},{16,80},{32,96},{48,112},{64,0},{80,16},{96,32},{112,48},{1... | collective-permute-start | bytes 540680 | tf_op jit(solution)/shard_map/ppermute | solution.py:41
  20.9 0.1 multiply_convert_fusion.2
  20.9 1.7 %collective-permute-start.11 = (f16[2,160,512]{2,1,0:T(8,128)(2,1)S(1)}, f16[2,160,512]{2,1,0:T(8,128)(2,1)S(1)}, u32[]{:S(2)}, u32[]{:S(2)}) collective-permute-start(f16[2,160,512]{2,1,0:T(8,128)(2,1)S(1)} %multiply_convert_fusion.2), channel_id=1, source_target_pairs={{0,192},{16,208},{32,224},{48,240},{64,128},{80,144},{96,160},{112... | collective-permute-start | bytes 983048 | tf_op jit(solution)/shard_map/ppermute | solution.py:41
  22.6 0.2 multiply_convert_fusion
  22.8 0.1 collective-permute-start.13
  22.9 0.4 collective-permute-start.12
  23.3 2.7 %product.5 = f32[4,512,512]{2,1,0:T(8,128)S(1)} custom-call(s32[1]{0:T(128)} %bitcast.4.me, bf16[384,8192]{1,0:T(8,128)(2,1)} %bitcast.93, bf16[384,512]{1,0:T(8,128)(2,1)} %bitcast.98, bf16[384,2048]{1,0:T(8,128)(2,1)S(1)} %get-tuple-element.178.mine, bf16[384,2048]{1,0:T(8,128)(2,1)S(1)} %collective-permute-done.10.theirs, ...), custom_call_target="tpu_custom_call" | custom-call | flops 1610612736 | tf_op jit(solution)/shard_map/product/pallas_call | solution.py:168
  26.0 0.1 fusion.29
  26.1 2.1 %collective-permute-done.11 = f16[2,160,512]{2,1,0:T(8,128)(2,1)S(1)} collective-permute-done((f16[2,160,512]{2,1,0:T(8,128)(2,1)S(1)}, f16[2,160,512]{2,1,0:T(8,128)(2,1)S(1)}, u32[]{:S(2)}, u32[]{:S(2)}) %collective-permute-start.11) | collective-permute-done | bytes 327712 | tf_op jit(solution)/shard_map/ppermute | solution.py:41
  28.1 1.6 %collective-permute-start.15 = (f16[176,512]{1,0:T(8,128)(2,1)S(1)}, f16[176,512]{1,0:T(8,128)(2,1)S(1)}, u32[]{:S(2)}, u32[]{:S(2)}) collective-permute-start(f16[176,512]{1,0:T(8,128)(2,1)S(1)} %get-tuple-element.209), channel_id=1, source_target_pairs={{0,192},{16,208},{32,224},{48,240},{64,128},{80,144},{96,160},{112... | collective-permute-start | bytes 540680 | tf_op jit(solution)/shard_map/ppermute | solution.py:41
  29.8 0.1 fusion.30
  29.8 2.8 %collective-permute-done.13 = f16[2,176,512]{2,1,0:T(8,128)(2,1)S(1)} collective-permute-done((f16[2,176,512]{2,1,0:T(8,128)(2,1)S(1)}, f16[2,176,512]{2,1,0:T(8,128)(2,1)S(1)}, u32[]{:S(2)}, u32[]{:S(2)}) %collective-permute-start.13) | collective-permute-done | bytes 360480 | tf_op jit(solution)/shard_map/ppermute | solution.py:41
  32.7 1.3 %collective-permute-start.26 = (f16[160,512]{1,0:T(8,128)(2,1)S(1)}, f16[160,512]{1,0:T(8,128)(2,1)S(1)}, u32[]{:S(2)}, u32[]{:S(2)}) collective-permute-start(f16[160,512]{1,0:T(8,128)(2,1)S(1)} %fusion.32), channel_id=1, source_target_pairs={{0,192},{16,208},{32,224},{48,240},{64,128},{80,144},{96,160},{112... | collective-permute-start | bytes 491528 | tf_op jit(solution)/shard_map/ppermute | solution.py:41
  34.0 0.0 collective-permute-done.12
  34.0 0.0 collective-permute-start.27
  34.0 0.1 fusion.25
  34.1 0.9 collective-permute-start.23
  35.0 0.1 fusion.23
  35.1 0.8 collective-permute-start.20
  35.9 1.4 %collective-permute-start.28 = (f16[160,512]{1,0:T(8,128)(2,1)S(1)}, f16[160,512]{1,0:T(8,128)(2,1)S(1)}, u32[]{:S(2)}, u32[]{:S(2)}) collective-permute-start(f16[160,512]{1,0:T(8,128)(2,1)S(1)} %fusion.23), channel_id=1, source_target_pairs={{0,64},{16,80},{32,96},{48,112},{64,0},{80,16},{96,32},{112,48},{1... | collective-permute-start | bytes 491528 | tf_op jit(solution)/shard_map/ppermute | solution.py:41
  37.3 0.2 fusion.11
  37.6 2.4 %hold.1 = (f32[512,512]{1,0:T(8,128)S(1)}, f32[512,512]{1,0:T(8,128)S(1)}, f32[512,512]{1,0:T(8,128)S(1)}, s32[1]{0:T(128)}) custom-call(s32[1]{0:T(128)S(6)} %copy.21.step_index, f32[512,512]{1,0:T(8,128)} %bitcast.99, f32[512,512]{1,0:T(8,128)} %bitcast.100, f32[512,512]{1,0:T(8,128)} %bitcast.101), custom_call_target="tpu_custom_call" | custom-call | tf_op jit(solution)/shard_map/hold/pallas_call | solution.py:125
  40.0 1.7 %collective-permute-start.22 = (f16[176,512]{1,0:T(8,128)(2,1)S(1)}, f16[176,512]{1,0:T(8,128)(2,1)S(1)}, u32[]{:S(2)}, u32[]{:S(2)}) collective-permute-start(f16[176,512]{1,0:T(8,128)(2,1)S(1)} %get-tuple-element.202), channel_id=1, source_target_pairs={{0,192},{16,208},{32,224},{48,240},{64,128},{80,144},{96,160},{112... | collective-permute-start | bytes 540680 | tf_op jit(solution)/shard_map/ppermute | solution.py:41
  41.6 0.2 collective-permute-start.25
  41.8 1.2 %collective-permute-start.24 = (f16[176,512]{1,0:T(8,128)(2,1)S(1)}, f16[176,512]{1,0:T(8,128)(2,1)S(1)}, u32[]{:S(2)}, u32[]{:S(2)}) collective-permute-start(f16[176,512]{1,0:T(8,128)(2,1)S(1)} %get-tuple-element.204), channel_id=1, source_target_pairs={{0,192},{16,208},{32,224},{48,240},{64,128},{80,144},{96,160},{112... | collective-permute-start | bytes 540680 | tf_op jit(solution)/shard_map/ppermute | solution.py:41
  43.0 0.1 fusion.19.refs_2_
  43.2 2.6 %collective-permute-done.22 = f16[176,512]{1,0:T(8,128)(2,1)S(1)} collective-permute-done((f16[176,512]{1,0:T(8,128)(2,1)S(1)}, f16[176,512]{1,0:T(8,128)(2,1)S(1)}, u32[]{:S(2)}, u32[]{:S(2)}) %collective-permute-start.22) | collective-permute-done | bytes 180256 | tf_op jit(solution)/shard_map/ppermute | solution.py:41
  45.8 0.2 collective-permute-done.25
  46.0 1.7 %collective-permute-done.24 = f16[176,512]{1,0:T(8,128)(2,1)S(1)} collective-permute-done((f16[176,512]{1,0:T(8,128)(2,1)S(1)}, f16[176,512]{1,0:T(8,128)(2,1)S(1)}, u32[]{:S(2)}, u32[]{:S(2)}) %collective-permute-start.24) | collective-permute-done | bytes 180256 | tf_op jit(solution)/shard_map/ppermute | solution.py:41
  47.7 0.2 fusion.5
  48.0 0.1 squares.1
  48.1 15.2 %all_to_all.5.all_squares = f32[16,1,128]{2,1,0:T(1,128)S(1)} all-to-all(f32[16,1,128]{2,1,0:T(1,128)S(1)} %squares.1), channel_id=1, replica_groups=mesh['fsdp'=16,'replica'=16] {'fsdp'}, dimensions={0} | all-to-all | bytes 16384 | tf_op jit(solution)/shard_map/all_to_all | solution.py:375
  63.3 0.4 adam.9
  63.7 25.9 %conditional.1 = (f32[512,512]{1,0:T(8,128)}, f32[512,512]{1,0:T(8,128)}, f32[1,512,512]{2,1,0:T(8,128)S(1)}) conditional(s32[]{:T(128)} %bitcast.25, (f32[8,512]{1,0:T(8,128)S(1)}, f32[176,512]{1,0:T(8,128)S(1)}, f32[176,512]{1,0:T(8,128)S(1)}, f32[160,512]{1,0:T(8,128)S(1)}, f32[512,512]{1,0:T(8,128)S(1)}, ...), branch_computations={%region_0.0_spmd, %region_1.0_spmd, %region_2.0_spmd, %region_3.0_... | conditional | flops 8560640 | bytes 17285224 | solution.py:379
  64.4 2.2 %collective-permute-start.4 = (f16[176,512]{1,0:T(8,128)(2,1)S(1)}, f16[176,512]{1,0:T(8,128)(2,1)S(1)}, u32[]{:S(2)}, u32[]{:S(2)}) collective-permute-start(f16[176,512]{1,0:T(8,128)(2,1)S(1)} %get-tuple-element.126), channel_id=1, source_target_pairs={{0,4},{1,5},{2,6},{3,7},{4,0},{5,1},{6,2},{7,3},{8,12},{9,13},{10,... | collective-permute-start | bytes 540680 | tf_op jit(solution)/shard_map/cond/branch_2_fun/ppermute | solution.py:45
  66.6 1.8 %adam.7 = (f32[336,512]{1,0:T(8,128)S(1)}, f32[8,512]{1,0:T(8,128)}) custom-call(s32[1]{0:T(128)} %get-tuple-element.127.step_index, f32[16,1,128]{2,1,0:T(1,128)S(1)} %get-tuple-element.128.all_squares, f32[176,512]{1,0:T(8,128)S(1)} %get-tuple-element.119.refs_1_.refs_0_, f32[160,512]{1,0:T(8,128)S(1)} %get-tuple-element.120.refs_2_.refs_1_, ...), custom_call_target="tpu_custom_call" | custom-call | flops 5242880 | bytes 4194304 | tf_op jit(solution)/shard_map/cond/branch_2_fun/adam/pallas_call | solution.py:235
  68.4 0.3 collective-permute-start.5
  68.8 1.6 %moments.6 = (f32[512,512]{1,0:T(8,128)}, f32[512,512]{1,0:T(8,128)}) custom-call(f32[8,512]{1,0:T(8,128)S(1)} %get-tuple-element.117.clip, f32[176,512]{1,0:T(8,128)S(1)} %get-tuple-element.118.refs_0_, f32[176,512]{1,0:T(8,128)S(1)} %get-tuple-element.119.refs_1_.refs_0_, f32[160,512]{1,0:T(8,128)S(1)} %get-tuple-element.120.refs_2_.refs_1_, ...), custom_call_target="tpu_custom_call" | custom-call | flops 2097152 | bytes 5242880 | tf_op jit(solution)/shard_map/cond/branch_2_fun/moments/pallas_call | solution.py:264
  70.4 11.7 %collective-permute-done.4 = f16[176,512]{1,0:T(8,128)(2,1)S(1)} collective-permute-done((f16[176,512]{1,0:T(8,128)(2,1)S(1)}, f16[176,512]{1,0:T(8,128)(2,1)S(1)}, u32[]{:S(2)}, u32[]{:S(2)}) %collective-permute-start.4) | collective-permute-done | bytes 180256 | tf_op jit(solution)/shard_map/cond/branch_2_fun/ppermute | solution.py:45
  82.1 0.1 add_multiply_fusion.5
  82.1 7.3 %collective-permute-done.5 = f16[336,512]{1,0:T(8,128)(2,1)S(1)} collective-permute-done((f16[336,512]{1,0:T(8,128)(2,1)S(1)}, f16[336,512]{1,0:T(8,128)(2,1)S(1)}, u32[]{:S(2)}, u32[]{:S(2)}) %collective-permute-start.5) | collective-permute-done | bytes 344096 | tf_op jit(solution)/shard_map/cond/branch_2_fun/ppermute | solution.py:45
  89.4 0.1 add_multiply_fusion.4
  89.5 0.1 maximum_bitcast_fusion.2
  89.6 0.0 copy-start
  89.6 1.0 %copy-done = f32[1,512,512]{2,1,0:T(8,128)} copy-done((f32[1,512,512]{2,1,0:T(8,128)}, f32[1,512,512]{2,1,0:T(8,128)S(1)}, u32[]{:S(2)}) %copy-start) | copy-done | bytes 1048600
  (15 shorter events, 0.2 us)
Async XLA Ops:
  1.8 5.3 %collective-permute-start.8 = (bf16[384,1024]{1,0:T(8,128)(2,1)S(1)}, bf16[384,1024]{1,0:T(8,128)(2,1)S(1)}, u32[]{:S(2)}, u32[]{:S(2)}) collective-permute-start(bf16[384,1024]{1,0:T(8,128)(2,1)S(1)} %fetch.3), channel_id=1, source_target_pairs={{0,16},{16,0},{32,48},{48,32},{64,80},{80,64},{96,112},{112,96},{1... | collective-permute-start | bytes 2359304 | tf_op jit(solution)/shard_map/ppermute | solution.py:41
  7.0 2.9 %collective-permute-start.9 = (bf16[384,1536]{1,0:T(8,128)(2,1)S(1)}, bf16[384,1536]{1,0:T(8,128)(2,1)S(1)}, u32[]{:S(2)}, u32[]{:S(2)}) collective-permute-start(bf16[384,1536]{1,0:T(8,128)(2,1)S(1)} %get-tuple-element.177), channel_id=1, source_target_pairs={{0,16},{16,0},{32,48},{48,32},{64,80},{80,64},{96,112},{112,96},{1... | collective-permute-start | bytes 3538952 | tf_op jit(solution)/shard_map/ppermute | solution.py:41
  12.0 11.0 %collective-permute-start.10 = (bf16[384,2048]{1,0:T(8,128)(2,1)S(1)}, bf16[384,2048]{1,0:T(8,128)(2,1)S(1)}, u32[]{:S(2)}, u32[]{:S(2)}) collective-permute-start(bf16[384,2048]{1,0:T(8,128)(2,1)S(1)} %get-tuple-element.179), channel_id=1, source_target_pairs={{0,16},{16,0},{32,48},{48,32},{64,80},{80,64},{96,112},{112,96},{1... | collective-permute-start | bytes 4718600 | tf_op jit(solution)/shard_map/ppermute | solution.py:41
  12.2 6.6 %collective-permute-start.16 = (f16[160,512]{1,0:T(8,128)(2,1)S(1)}, f16[160,512]{1,0:T(8,128)(2,1)S(1)}, u32[]{:S(2)}, u32[]{:S(2)}) collective-permute-start(f16[160,512]{1,0:T(8,128)(2,1)S(1)} %fusion.31), channel_id=1, source_target_pairs={{0,192},{16,208},{32,224},{48,240},{64,128},{80,144},{96,160},{112... | collective-permute-start | bytes 491528 | tf_op jit(solution)/shard_map/ppermute | solution.py:41
  13.9 5.5 %collective-permute-start.14 = (f16[176,512]{1,0:T(8,128)(2,1)S(1)}, f16[176,512]{1,0:T(8,128)(2,1)S(1)}, u32[]{:S(2)}, u32[]{:S(2)}) collective-permute-start(f16[176,512]{1,0:T(8,128)(2,1)S(1)} %get-tuple-element.212), channel_id=1, source_target_pairs={{0,64},{16,80},{32,96},{48,112},{64,0},{80,16},{96,32},{112,48},{1... | collective-permute-start | bytes 540680 | tf_op jit(solution)/shard_map/ppermute | solution.py:41
  14.0 5.5 %collective-permute-start.18 = (f16[176,512]{1,0:T(8,128)(2,1)S(1)}, f16[176,512]{1,0:T(8,128)(2,1)S(1)}, u32[]{:S(2)}, u32[]{:S(2)}) collective-permute-start(f16[176,512]{1,0:T(8,128)(2,1)S(1)} %get-tuple-element.213), channel_id=1, source_target_pairs={{0,32},{16,48},{32,0},{48,16},{64,96},{80,112},{96,64},{112,80},{1... | collective-permute-start | bytes 540680 | tf_op jit(solution)/shard_map/ppermute | solution.py:41
  18.9 15.3 %collective-permute-start.17 = (f16[160,512]{1,0:T(8,128)(2,1)S(1)}, f16[160,512]{1,0:T(8,128)(2,1)S(1)}, u32[]{:S(2)}, u32[]{:S(2)}) collective-permute-start(f16[160,512]{1,0:T(8,128)(2,1)S(1)} %fusion.21), channel_id=1, source_target_pairs={{0,32},{16,48},{32,0},{48,16},{64,96},{80,112},{96,64},{112,80},{1... | collective-permute-start | bytes 491528 | tf_op jit(solution)/shard_map/ppermute | solution.py:41
  19.7 15.5 %collective-permute-start.19 = (f16[176,512]{1,0:T(8,128)(2,1)S(1)}, f16[176,512]{1,0:T(8,128)(2,1)S(1)}, u32[]{:S(2)}, u32[]{:S(2)}) collective-permute-start(f16[176,512]{1,0:T(8,128)(2,1)S(1)} %get-tuple-element.208), channel_id=1, source_target_pairs={{0,64},{16,80},{32,96},{48,112},{64,0},{80,16},{96,32},{112,48},{1... | collective-permute-start | bytes 540680 | tf_op jit(solution)/shard_map/ppermute | solution.py:41
  20.9 7.2 %collective-permute-start.11 = (f16[2,160,512]{2,1,0:T(8,128)(2,1)S(1)}, f16[2,160,512]{2,1,0:T(8,128)(2,1)S(1)}, u32[]{:S(2)}, u32[]{:S(2)}) collective-permute-start(f16[2,160,512]{2,1,0:T(8,128)(2,1)S(1)} %multiply_convert_fusion.2), channel_id=1, source_target_pairs={{0,192},{16,208},{32,224},{48,240},{64,128},{80,144},{96,160},{112... | collective-permute-start | bytes 983048 | tf_op jit(solution)/shard_map/ppermute | solution.py:41
  22.8 9.9 %collective-permute-start.13 = (f16[2,176,512]{2,1,0:T(8,128)(2,1)S(1)}, f16[2,176,512]{2,1,0:T(8,128)(2,1)S(1)}, u32[]{:S(2)}, u32[]{:S(2)}) collective-permute-start(f16[2,176,512]{2,1,0:T(8,128)(2,1)S(1)} %get-tuple-element.210), channel_id=1, source_target_pairs={{0,64},{16,80},{32,96},{48,112},{64,0},{80,16},{96,32},{112,48},{1... | collective-permute-start | bytes 1081352 | tf_op jit(solution)/shard_map/ppermute | solution.py:41
  22.9 11.0 %collective-permute-start.12 = (f16[2,176,512]{2,1,0:T(8,128)(2,1)S(1)}, f16[2,176,512]{2,1,0:T(8,128)(2,1)S(1)}, u32[]{:S(2)}, u32[]{:S(2)}) collective-permute-start(f16[2,176,512]{2,1,0:T(8,128)(2,1)S(1)} %get-tuple-element.211), channel_id=1, source_target_pairs={{0,32},{16,48},{32,0},{48,16},{64,96},{80,112},{96,64},{112,80},{1... | collective-permute-start | bytes 1081352 | tf_op jit(solution)/shard_map/ppermute | solution.py:41
  28.1 7.8 %collective-permute-start.15 = (f16[176,512]{1,0:T(8,128)(2,1)S(1)}, f16[176,512]{1,0:T(8,128)(2,1)S(1)}, u32[]{:S(2)}, u32[]{:S(2)}) collective-permute-start(f16[176,512]{1,0:T(8,128)(2,1)S(1)} %get-tuple-element.209), channel_id=1, source_target_pairs={{0,192},{16,208},{32,224},{48,240},{64,128},{80,144},{96,160},{112... | collective-permute-start | bytes 540680 | tf_op jit(solution)/shard_map/ppermute | solution.py:41
  32.7 7.3 %collective-permute-start.26 = (f16[160,512]{1,0:T(8,128)(2,1)S(1)}, f16[160,512]{1,0:T(8,128)(2,1)S(1)}, u32[]{:S(2)}, u32[]{:S(2)}) collective-permute-start(f16[160,512]{1,0:T(8,128)(2,1)S(1)} %fusion.32), channel_id=1, source_target_pairs={{0,192},{16,208},{32,224},{48,240},{64,128},{80,144},{96,160},{112... | collective-permute-start | bytes 491528 | tf_op jit(solution)/shard_map/ppermute | solution.py:41
  34.0 7.7 %collective-permute-start.27 = (f16[160,512]{1,0:T(8,128)(2,1)S(1)}, f16[160,512]{1,0:T(8,128)(2,1)S(1)}, u32[]{:S(2)}, u32[]{:S(2)}) collective-permute-start(f16[160,512]{1,0:T(8,128)(2,1)S(1)} %fusion.30), channel_id=1, source_target_pairs={{0,32},{16,48},{32,0},{48,16},{64,96},{80,112},{96,64},{112,80},{1... | collective-permute-start | bytes 491528 | tf_op jit(solution)/shard_map/ppermute | solution.py:41
  34.1 8.9 %collective-permute-start.23 = (f16[176,512]{1,0:T(8,128)(2,1)S(1)}, f16[176,512]{1,0:T(8,128)(2,1)S(1)}, u32[]{:S(2)}, u32[]{:S(2)}) collective-permute-start(f16[176,512]{1,0:T(8,128)(2,1)S(1)} %get-tuple-element.206), channel_id=1, source_target_pairs={{0,64},{16,80},{32,96},{48,112},{64,0},{80,16},{96,32},{112,48},{1... | collective-permute-start | bytes 540680 | tf_op jit(solution)/shard_map/ppermute | solution.py:41
  35.1 8.0 %collective-permute-start.20 = (f16[176,512]{1,0:T(8,128)(2,1)S(1)}, f16[176,512]{1,0:T(8,128)(2,1)S(1)}, u32[]{:S(2)}, u32[]{:S(2)}) collective-permute-start(f16[176,512]{1,0:T(8,128)(2,1)S(1)} %get-tuple-element.207), channel_id=1, source_target_pairs={{0,32},{16,48},{32,0},{48,16},{64,96},{80,112},{96,64},{112,80},{1... | collective-permute-start | bytes 540680 | tf_op jit(solution)/shard_map/ppermute | solution.py:41
  35.9 5.9 %collective-permute-start.28 = (f16[160,512]{1,0:T(8,128)(2,1)S(1)}, f16[160,512]{1,0:T(8,128)(2,1)S(1)}, u32[]{:S(2)}, u32[]{:S(2)}) collective-permute-start(f16[160,512]{1,0:T(8,128)(2,1)S(1)} %fusion.23), channel_id=1, source_target_pairs={{0,64},{16,80},{32,96},{48,112},{64,0},{80,16},{96,32},{112,48},{1... | collective-permute-start | bytes 491528 | tf_op jit(solution)/shard_map/ppermute | solution.py:41
  40.0 5.8 %collective-permute-start.22 = (f16[176,512]{1,0:T(8,128)(2,1)S(1)}, f16[176,512]{1,0:T(8,128)(2,1)S(1)}, u32[]{:S(2)}, u32[]{:S(2)}) collective-permute-start(f16[176,512]{1,0:T(8,128)(2,1)S(1)} %get-tuple-element.202), channel_id=1, source_target_pairs={{0,192},{16,208},{32,224},{48,240},{64,128},{80,144},{96,160},{112... | collective-permute-start | bytes 540680 | tf_op jit(solution)/shard_map/ppermute | solution.py:41
  41.6 4.3 %collective-permute-start.25 = (f16[176,512]{1,0:T(8,128)(2,1)S(1)}, f16[176,512]{1,0:T(8,128)(2,1)S(1)}, u32[]{:S(2)}, u32[]{:S(2)}) collective-permute-start(f16[176,512]{1,0:T(8,128)(2,1)S(1)} %get-tuple-element.203), channel_id=1, source_target_pairs={{0,32},{16,48},{32,0},{48,16},{64,96},{80,112},{96,64},{112,80},{1... | collective-permute-start | bytes 540680 | tf_op jit(solution)/shard_map/ppermute | solution.py:41
  41.8 5.9 %collective-permute-start.24 = (f16[176,512]{1,0:T(8,128)(2,1)S(1)}, f16[176,512]{1,0:T(8,128)(2,1)S(1)}, u32[]{:S(2)}, u32[]{:S(2)}) collective-permute-start(f16[176,512]{1,0:T(8,128)(2,1)S(1)} %get-tuple-element.204), channel_id=1, source_target_pairs={{0,192},{16,208},{32,224},{48,240},{64,128},{80,144},{96,160},{112... | collective-permute-start | bytes 540680 | tf_op jit(solution)/shard_map/ppermute | solution.py:41
  43.0 4.7 %collective-permute-start.21 = (f16[176,512]{1,0:T(8,128)(2,1)S(1)}, f16[176,512]{1,0:T(8,128)(2,1)S(1)}, u32[]{:S(2)}, u32[]{:S(2)}) collective-permute-start(f16[176,512]{1,0:T(8,128)(2,1)S(1)} %get-tuple-element.205), channel_id=1, source_target_pairs={{0,64},{16,80},{32,96},{48,112},{64,0},{80,16},{96,32},{112,48},{1... | collective-permute-start | bytes 540680 | tf_op jit(solution)/shard_map/ppermute | solution.py:41
  64.4 17.7 %collective-permute-start.4 = (f16[176,512]{1,0:T(8,128)(2,1)S(1)}, f16[176,512]{1,0:T(8,128)(2,1)S(1)}, u32[]{:S(2)}, u32[]{:S(2)}) collective-permute-start(f16[176,512]{1,0:T(8,128)(2,1)S(1)} %get-tuple-element.126), channel_id=1, source_target_pairs={{0,4},{1,5},{2,6},{3,7},{4,0},{5,1},{6,2},{7,3},{8,12},{9,13},{10,... | collective-permute-start | bytes 540680 | tf_op jit(solution)/shard_map/cond/branch_2_fun/ppermute | solution.py:45
  68.4 21.0 %collective-permute-start.5 = (f16[336,512]{1,0:T(8,128)(2,1)S(1)}, f16[336,512]{1,0:T(8,128)(2,1)S(1)}, u32[]{:S(2)}, u32[]{:S(2)}) collective-permute-start(f16[336,512]{1,0:T(8,128)(2,1)S(1)} %convert_element_type.126), channel_id=1, source_target_pairs={{0,4},{1,5},{2,6},{3,7},{4,0},{5,1},{6,2},{7,3},{8,12},{9,13},{10,... | collective-permute-start | bytes 1032200 | tf_op jit(solution)/shard_map/cond/branch_2_fun/ppermute | solution.py:45
  89.6 1.0 %copy-start = (f32[1,512,512]{2,1,0:T(8,128)}, f32[1,512,512]{2,1,0:T(8,128)S(1)}, u32[]{:S(2)}) copy-start(f32[1,512,512]{2,1,0:T(8,128)S(1)} %get-tuple-element.171) | copy-start | bytes 3145732

commit v3 on v2

--- a/solution.py
+++ b/solution.py
@@ -276,10 +276,16 @@
 
 def finish(apart, packed, updated, clip, pieces, weights, first, second, step_index, all_squares):
     f32 = jnp.float32
-    theirs = from_partner(apart, packed)
     start = packed.shape[0]
+    if apart < 3:
+        theirs = from_partner(apart, packed)
     behind, _ = adam(start, step_index, all_squares, pieces[1:], weights, first, second)
-    theirs_behind = from_partner(apart, behind.astype(jnp.float16))
+    packed_behind = behind.astype(jnp.float16)
+    if apart < 3:
+        theirs_behind = from_partner(apart, packed_behind)
+    else:
+        both = from_partner(apart, jnp.concatenate([packed, packed_behind]))
+        theirs, theirs_behind = both[:start], both[start:]
     new_first, new_second = moments(clip, pieces, first, second)
     new_weights = jnp.concatenate(
         [0.5 * (updated + theirs.astype(f32)), 0.5 * (behind + theirs_behind.astype(f32))]

time: 90.8 us -> 90.8 us (level)
  no operation moved by 1% of the time
where the time goes in v3:
time: 90.8 us; the launch traced here: 90.6 us
  waiting for transfers between devices  34.6 us (38%)
  starting transfers between devices  21.1 us (23%)
  blocking collectives  15.2 us (17%)
  Pallas kernels  14.7 us (16%)
  other arithmetic  1.79 us (2%)
  between operations  1.51 us (2%)
  local copies, waits for them, and re-layouts  0.96 us (1%)
    ppermute x2, waiting for transfers between devices, from_partner(): lax.ppermute(array, 'replica', [(i, i ^ 1 << apart) for i in range(16)])  19 us
    ppermute x21, starting transfers between devices, exchange(): lax.ppermute(array, 'fsdp', [(i, neighbour(i, dim)) for i in range(16)])  18.6 us
    ppermute x21, waiting for transfers between devices, exchange(): lax.ppermute(array, 'fsdp', [(i, neighbour(i, dim)) for i in range(16)])  15.6 us
    all_to_all x1, blocking collectives, local(): all_squares = lax.all_to_all(squares_of(pieces), 'fsdp', 0, 0, tiled=True)  15.2 us
    pallas_call x3, Pallas kernels, product(): pl.pallas_call(partial(product_kernel, wanted), in_specs=[smem, hbm, hbm]...  5.33 us
    pallas_call x2, Pallas kernels, fetch(): pl.pallas_call(partial(fetch_kernel, wanted), in_specs=[pl.BlockSpec(memo...  3.11 us
    ppermute x2, starting transfers between devices, from_partner(): lax.ppermute(array, 'replica', [(i, i ^ 1 << apart) for i in range(16)])  2.54 us
    pallas_call x1, Pallas kernels, hold(): pl.pallas_call(hold_kernel, in_specs=[pl.BlockSpec(memory_space=pltpu.SME...  2.41 us
  transfers between devices with their start and end apart: 23, of which 11 were waited for; matrix products, arithmetic and copies ran while one was open for 2% of the time, Pallas kernels for 12%

profile of v3, /device:TPU:1, one launch (start us, length us, event | category | flops | bytes accessed | tf_op | source)
XLA Modules:
  0.0 90.6 jit_solution(9710102743919828874)
XLA Ops:
  0.6 1.2 %fetch.3 = bf16[384,1024]{1,0:T(8,128)(2,1)S(1)} custom-call(s32[1]{0:T(128)} %bitcast.4.me, bf16[384,8192]{1,0:T(8,128)(2,1)} %bitcast.89, bf16[384,512]{1,0:T(8,128)(2,1)} %bitcast.94), custom_call_target="tpu_custom_call" | custom-call | bytes 1572864 | tf_op jit(solution)/shard_map/fetch/pallas_call | solution.py:92
  1.8 3.3 %collective-permute-start.7 = (bf16[384,1024]{1,0:T(8,128)(2,1)S(1)}, bf16[384,1024]{1,0:T(8,128)(2,1)S(1)}, u32[]{:S(2)}, u32[]{:S(2)}) collective-permute-start(bf16[384,1024]{1,0:T(8,128)(2,1)S(1)} %fetch.3), channel_id=1, source_target_pairs={{0,16},{16,0},{32,48},{48,32},{64,80},{80,64},{96,112},{112,96},{1... | collective-permute-start | bytes 2359304 | tf_op jit(solution)/shard_map/ppermute | solution.py:41
  5.1 1.9 %fetch.2 = (bf16[384,1536]{1,0:T(8,128)(2,1)S(1)}, bf16[384,1024]{1,0:T(8,128)(2,1)S(1)}, bf16[384,1536]{1,0:T(8,128)(2,1)S(1)}) custom-call(s32[1]{0:T(128)} %bitcast.4.me, bf16[384,8192]{1,0:T(8,128)(2,1)} %bitcast.90, bf16[384,512]{1,0:T(8,128)(2,1)} %bitcast.95), custom_call_target="tpu_custom_call" | custom-call | bytes 6291456 | tf_op jit(solution)/shard_map/fetch/pallas_call | solution.py:92
  7.0 0.1 collective-permute-start.8
  7.2 0.0 collective-permute-done.7.theirs.g_theirs
  7.2 0.7 product.3
  7.9 0.1 fusion.27
  8.0 2.0 %collective-permute-done.8.theirs = bf16[384,1536]{1,0:T(8,128)(2,1)S(1)} collective-permute-done((bf16[384,1536]{1,0:T(8,128)(2,1)S(1)}, bf16[384,1536]{1,0:T(8,128)(2,1)S(1)}, u32[]{:S(2)}, u32[]{:S(2)}) %collective-permute-start.8) | collective-permute-done | bytes 1179680 | tf_op jit(solution)/shard_map/ppermute | solution.py:41
  10.0 2.0 %product.4 = (f32[3,512,512]{2,1,0:T(8,128)S(1)}, bf16[384,2048]{1,0:T(8,128)(2,1)S(1)}, bf16[384,2048]{1,0:T(8,128)(2,1)S(1)}) custom-call(s32[1]{0:T(128)} %bitcast.4.me, bf16[384,8192]{1,0:T(8,128)(2,1)} %bitcast.92, bf16[384,512]{1,0:T(8,128)(2,1)} %bitcast.97, bf16[384,1536]{1,0:T(8,128)(2,1)S(1)} %get-tuple-element.176.mine, ...), custom_call_target="tpu_custom_call" | custom-call | flops 1207959552 | bytes 6291456 | tf_op jit(solution)/shard_map/product/pallas_call | solution.py:168
  12.0 0.2 collective-permute-start.9
  12.2 1.0 %collective-permute-start.15 = (f16[160,512]{1,0:T(8,128)(2,1)S(1)}, f16[160,512]{1,0:T(8,128)(2,1)S(1)}, u32[]{:S(2)}, u32[]{:S(2)}) collective-permute-start(f16[160,512]{1,0:T(8,128)(2,1)S(1)} %fusion.31), channel_id=1, source_target_pairs={{0,192},{16,208},{32,224},{48,240},{64,128},{80,144},{96,160},{112... | collective-permute-start | bytes 491528 | tf_op jit(solution)/shard_map/ppermute | solution.py:41
  13.9 0.1 collective-permute-start.13
  14.0 1.3 %collective-permute-start.17 = (f16[176,512]{1,0:T(8,128)(2,1)S(1)}, f16[176,512]{1,0:T(8,128)(2,1)S(1)}, u32[]{:S(2)}, u32[]{:S(2)}) collective-permute-start(f16[176,512]{1,0:T(8,128)(2,1)S(1)} %get-tuple-element.213), channel_id=1, source_target_pairs={{0,32},{16,48},{32,0},{48,16},{64,96},{80,112},{96,64},{112,80},{1... | collective-permute-start | bytes 540680 | tf_op jit(solution)/shard_map/ppermute | solution.py:41
  15.3 3.5 %collective-permute-done.15 = f16[160,512]{1,0:T(8,128)(2,1)S(1)} collective-permute-done((f16[160,512]{1,0:T(8,128)(2,1)S(1)}, f16[160,512]{1,0:T(8,128)(2,1)S(1)}, u32[]{:S(2)}, u32[]{:S(2)}) %collective-permute-start.15) | collective-permute-done | bytes 163872 | tf_op jit(solution)/shard_map/ppermute | solution.py:41
  18.8 0.1 fusion.21
  18.9 0.1 collective-permute-start.16
  19.0 0.5 collective-permute-done.13
  19.4 0.1 collective-permute-done.17
  19.5 0.1 fusion.9
  19.7 1.2 %collective-permute-start.18 = (f16[176,512]{1,0:T(8,128)(2,1)S(1)}, f16[176,512]{1,0:T(8,128)(2,1)S(1)}, u32[]{:S(2)}, u32[]{:S(2)}) collective-permute-start(f16[176,512]{1,0:T(8,128)(2,1)S(1)} %get-tuple-element.208), channel_id=1, source_target_pairs={{0,64},{16,80},{32,96},{48,112},{64,0},{80,16},{96,32},{112,48},{1... | collective-permute-start | bytes 540680 | tf_op jit(solution)/shard_map/ppermute | solution.py:41
  20.9 0.1 multiply_convert_fusion.2
  20.9 1.7 %collective-permute-start.10 = (f16[2,160,512]{2,1,0:T(8,128)(2,1)S(1)}, f16[2,160,512]{2,1,0:T(8,128)(2,1)S(1)}, u32[]{:S(2)}, u32[]{:S(2)}) collective-permute-start(f16[2,160,512]{2,1,0:T(8,128)(2,1)S(1)} %multiply_convert_fusion.2), channel_id=1, source_target_pairs={{0,192},{16,208},{32,224},{48,240},{64,128},{80,144},{96,160},{112... | collective-permute-start | bytes 983048 | tf_op jit(solution)/shard_map/ppermute | solution.py:41
  22.6 0.2 multiply_convert_fusion
  22.8 0.1 collective-permute-start.12
  22.9 0.4 collective-permute-start.11
  23.3 2.7 %product.5 = f32[4,512,512]{2,1,0:T(8,128)S(1)} custom-call(s32[1]{0:T(128)} %bitcast.4.me, bf16[384,8192]{1,0:T(8,128)(2,1)} %bitcast.93, bf16[384,512]{1,0:T(8,128)(2,1)} %bitcast.98, bf16[384,2048]{1,0:T(8,128)(2,1)S(1)} %get-tuple-element.178.mine, bf16[384,2048]{1,0:T(8,128)(2,1)S(1)} %collective-permute-done.9.theirs, ...), custom_call_target="tpu_custom_call" | custom-call | flops 1610612736 | tf_op jit(solution)/shard_map/product/pallas_call | solution.py:168
  26.0 0.1 fusion.29
  26.1 2.1 %collective-permute-done.10 = f16[2,160,512]{2,1,0:T(8,128)(2,1)S(1)} collective-permute-done((f16[2,160,512]{2,1,0:T(8,128)(2,1)S(1)}, f16[2,160,512]{2,1,0:T(8,128)(2,1)S(1)}, u32[]{:S(2)}, u32[]{:S(2)}) %collective-permute-start.10) | collective-permute-done | bytes 327712 | tf_op jit(solution)/shard_map/ppermute | solution.py:41
  28.1 1.6 %collective-permute-start.14 = (f16[176,512]{1,0:T(8,128)(2,1)S(1)}, f16[176,512]{1,0:T(8,128)(2,1)S(1)}, u32[]{:S(2)}, u32[]{:S(2)}) collective-permute-start(f16[176,512]{1,0:T(8,128)(2,1)S(1)} %get-tuple-element.209), channel_id=1, source_target_pairs={{0,192},{16,208},{32,224},{48,240},{64,128},{80,144},{96,160},{112... | collective-permute-start | bytes 540680 | tf_op jit(solution)/shard_map/ppermute | solution.py:41
  29.8 0.1 fusion.30
  29.8 2.8 %collective-permute-done.12 = f16[2,176,512]{2,1,0:T(8,128)(2,1)S(1)} collective-permute-done((f16[2,176,512]{2,1,0:T(8,128)(2,1)S(1)}, f16[2,176,512]{2,1,0:T(8,128)(2,1)S(1)}, u32[]{:S(2)}, u32[]{:S(2)}) %collective-permute-start.12) | collective-permute-done | bytes 360480 | tf_op jit(solution)/shard_map/ppermute | solution.py:41
  32.7 1.3 %collective-permute-start.25 = (f16[160,512]{1,0:T(8,128)(2,1)S(1)}, f16[160,512]{1,0:T(8,128)(2,1)S(1)}, u32[]{:S(2)}, u32[]{:S(2)}) collective-permute-start(f16[160,512]{1,0:T(8,128)(2,1)S(1)} %fusion.32), channel_id=1, source_target_pairs={{0,192},{16,208},{32,224},{48,240},{64,128},{80,144},{96,160},{112... | collective-permute-start | bytes 491528 | tf_op jit(solution)/shard_map/ppermute | solution.py:41
  34.0 0.0 collective-permute-done.11
  34.0 0.0 collective-permute-start.26
  34.0 0.1 fusion.25
  34.1 0.9 collective-permute-start.22
  35.0 0.1 fusion.23
  35.1 0.8 collective-permute-start.19
  35.9 1.4 %collective-permute-start.27 = (f16[160,512]{1,0:T(8,128)(2,1)S(1)}, f16[160,512]{1,0:T(8,128)(2,1)S(1)}, u32[]{:S(2)}, u32[]{:S(2)}) collective-permute-start(f16[160,512]{1,0:T(8,128)(2,1)S(1)} %fusion.23), channel_id=1, source_target_pairs={{0,64},{16,80},{32,96},{48,112},{64,0},{80,16},{96,32},{112,48},{1... | collective-permute-start | bytes 491528 | tf_op jit(solution)/shard_map/ppermute | solution.py:41
  37.3 0.2 fusion.11
  37.6 2.4 %hold.1 = (f32[512,512]{1,0:T(8,128)S(1)}, f32[512,512]{1,0:T(8,128)S(1)}, f32[512,512]{1,0:T(8,128)S(1)}, s32[1]{0:T(128)}) custom-call(s32[1]{0:T(128)S(6)} %copy.21.step_index, f32[512,512]{1,0:T(8,128)} %bitcast.99, f32[512,512]{1,0:T(8,128)} %bitcast.100, f32[512,512]{1,0:T(8,128)} %bitcast.101), custom_call_target="tpu_custom_call" | custom-call | tf_op jit(solution)/shard_map/hold/pallas_call | solution.py:125
  40.0 1.7 %collective-permute-start.21 = (f16[176,512]{1,0:T(8,128)(2,1)S(1)}, f16[176,512]{1,0:T(8,128)(2,1)S(1)}, u32[]{:S(2)}, u32[]{:S(2)}) collective-permute-start(f16[176,512]{1,0:T(8,128)(2,1)S(1)} %get-tuple-element.202), channel_id=1, source_target_pairs={{0,192},{16,208},{32,224},{48,240},{64,128},{80,144},{96,160},{112... | collective-permute-start | bytes 540680 | tf_op jit(solution)/shard_map/ppermute | solution.py:41
  41.6 0.2 collective-permute-start.24
  41.8 1.2 %collective-permute-start.23 = (f16[176,512]{1,0:T(8,128)(2,1)S(1)}, f16[176,512]{1,0:T(8,128)(2,1)S(1)}, u32[]{:S(2)}, u32[]{:S(2)}) collective-permute-start(f16[176,512]{1,0:T(8,128)(2,1)S(1)} %get-tuple-element.204), channel_id=1, source_target_pairs={{0,192},{16,208},{32,224},{48,240},{64,128},{80,144},{96,160},{112... | collective-permute-start | bytes 540680 | tf_op jit(solution)/shard_map/ppermute | solution.py:41
  43.0 0.1 fusion.19.refs_2_
  43.2 2.6 %collective-permute-done.21 = f16[176,512]{1,0:T(8,128)(2,1)S(1)} collective-permute-done((f16[176,512]{1,0:T(8,128)(2,1)S(1)}, f16[176,512]{1,0:T(8,128)(2,1)S(1)}, u32[]{:S(2)}, u32[]{:S(2)}) %collective-permute-start.21) | collective-permute-done | bytes 180256 | tf_op jit(solution)/shard_map/ppermute | solution.py:41
  45.8 0.2 collective-permute-done.24
  46.0 1.7 %collective-permute-done.23 = f16[176,512]{1,0:T(8,128)(2,1)S(1)} collective-permute-done((f16[176,512]{1,0:T(8,128)(2,1)S(1)}, f16[176,512]{1,0:T(8,128)(2,1)S(1)}, u32[]{:S(2)}, u32[]{:S(2)}) %collective-permute-start.23) | collective-permute-done | bytes 180256 | tf_op jit(solution)/shard_map/ppermute | solution.py:41
  47.7 0.2 fusion.5
  48.0 0.1 squares.1
  48.1 15.2 %all_to_all.5.all_squares = f32[16,1,128]{2,1,0:T(1,128)S(1)} all-to-all(f32[16,1,128]{2,1,0:T(1,128)S(1)} %squares.1), channel_id=1, replica_groups=mesh['fsdp'=16,'replica'=16] {'fsdp'}, dimensions={0} | all-to-all | bytes 16384 | tf_op jit(solution)/shard_map/all_to_all | solution.py:381
  63.3 0.4 adam.9
  63.7 25.9 %conditional.1 = (f32[512,512]{1,0:T(8,128)}, f32[512,512]{1,0:T(8,128)}, f32[1,512,512]{2,1,0:T(8,128)S(1)}) conditional(s32[]{:T(128)} %bitcast.25, (f32[8,512]{1,0:T(8,128)S(1)}, f32[176,512]{1,0:T(8,128)S(1)}, f32[176,512]{1,0:T(8,128)S(1)}, f32[160,512]{1,0:T(8,128)S(1)}, f32[512,512]{1,0:T(8,128)S(1)}, ...), branch_computations={%region_0.0_spmd, %region_1.0_spmd, %region_2.0_spmd, %region_3.0_... | conditional | flops 8822784 | bytes 18333760 | solution.py:385
  64.4 2.2 %collective-permute-start.4 = (f16[176,512]{1,0:T(8,128)(2,1)S(1)}, f16[176,512]{1,0:T(8,128)(2,1)S(1)}, u32[]{:S(2)}, u32[]{:S(2)}) collective-permute-start(f16[176,512]{1,0:T(8,128)(2,1)S(1)} %get-tuple-element.126), channel_id=1, source_target_pairs={{0,4},{1,5},{2,6},{3,7},{4,0},{5,1},{6,2},{7,3},{8,12},{9,13},{10,... | collective-permute-start | bytes 540680 | tf_op jit(solution)/shard_map/cond/branch_2_fun/ppermute | solution.py:45
  66.6 1.8 %adam.7 = (f32[336,512]{1,0:T(8,128)S(1)}, f32[8,512]{1,0:T(8,128)}) custom-call(s32[1]{0:T(128)} %get-tuple-element.127.step_index, f32[16,1,128]{2,1,0:T(1,128)S(1)} %get-tuple-element.128.all_squares, f32[176,512]{1,0:T(8,128)S(1)} %get-tuple-element.119.refs_1_.refs_0_, f32[160,512]{1,0:T(8,128)S(1)} %get-tuple-element.120.refs_2_.refs_1_, ...), custom_call_target="tpu_custom_call" | custom-call | flops 5242880 | bytes 4194304 | tf_op jit(solution)/shard_map/cond/branch_2_fun/adam/pallas_call | solution.py:235
  68.4 0.3 collective-permute-start.5
  68.8 1.6 %moments.6 = (f32[512,512]{1,0:T(8,128)}, f32[512,512]{1,0:T(8,128)}) custom-call(f32[8,512]{1,0:T(8,128)S(1)} %get-tuple-element.117.clip, f32[176,512]{1,0:T(8,128)S(1)} %get-tuple-element.118.refs_0_, f32[176,512]{1,0:T(8,128)S(1)} %get-tuple-element.119.refs_1_.refs_0_, f32[160,512]{1,0:T(8,128)S(1)} %get-tuple-element.120.refs_2_.refs_1_, ...), custom_call_target="tpu_custom_call" | custom-call | flops 2097152 | bytes 5242880 | tf_op jit(solution)/shard_map/cond/branch_2_fun/moments/pallas_call | solution.py:264
  70.4 11.7 %collective-permute-done.4 = f16[176,512]{1,0:T(8,128)(2,1)S(1)} collective-permute-done((f16[176,512]{1,0:T(8,128)(2,1)S(1)}, f16[176,512]{1,0:T(8,128)(2,1)S(1)}, u32[]{:S(2)}, u32[]{:S(2)}) %collective-permute-start.4) | collective-permute-done | bytes 180256 | tf_op jit(solution)/shard_map/cond/branch_2_fun/ppermute | solution.py:45
  82.1 0.1 add_multiply_fusion.5
  82.1 7.3 %collective-permute-done.5 = f16[336,512]{1,0:T(8,128)(2,1)S(1)} collective-permute-done((f16[336,512]{1,0:T(8,128)(2,1)S(1)}, f16[336,512]{1,0:T(8,128)(2,1)S(1)}, u32[]{:S(2)}, u32[]{:S(2)}) %collective-permute-start.5) | collective-permute-done | bytes 344096 | tf_op jit(solution)/shard_map/cond/branch_2_fun/ppermute | solution.py:45
  89.4 0.1 add_multiply_fusion.4
  89.5 0.1 maximum_bitcast_fusion.2
  89.6 0.0 copy-start
  89.6 1.0 %copy-done = f32[1,512,512]{2,1,0:T(8,128)} copy-done((f32[1,512,512]{2,1,0:T(8,128)}, f32[1,512,512]{2,1,0:T(8,128)S(1)}, u32[]{:S(2)}) %copy-start) | copy-done | bytes 1048600
  (15 shorter events, 0.2 us)
Async XLA Ops:
  1.8 5.3 %collective-permute-start.7 = (bf16[384,1024]{1,0:T(8,128)(2,1)S(1)}, bf16[384,1024]{1,0:T(8,128)(2,1)S(1)}, u32[]{:S(2)}, u32[]{:S(2)}) collective-permute-start(bf16[384,1024]{1,0:T(8,128)(2,1)S(1)} %fetch.3), channel_id=1, source_target_pairs={{0,16},{16,0},{32,48},{48,32},{64,80},{80,64},{96,112},{112,96},{1... | collective-permute-start | bytes 2359304 | tf_op jit(solution)/shard_map/ppermute | solution.py:41
  7.0 2.9 %collective-permute-start.8 = (bf16[384,1536]{1,0:T(8,128)(2,1)S(1)}, bf16[384,1536]{1,0:T(8,128)(2,1)S(1)}, u32[]{:S(2)}, u32[]{:S(2)}) collective-permute-start(bf16[384,1536]{1,0:T(8,128)(2,1)S(1)} %get-tuple-element.177), channel_id=1, source_target_pairs={{0,16},{16,0},{32,48},{48,32},{64,80},{80,64},{96,112},{112,96},{1... | collective-permute-start | bytes 3538952 | tf_op jit(solution)/shard_map/ppermute | solution.py:41
  12.0 11.0 %collective-permute-start.9 = (bf16[384,2048]{1,0:T(8,128)(2,1)S(1)}, bf16[384,2048]{1,0:T(8,128)(2,1)S(1)}, u32[]{:S(2)}, u32[]{:S(2)}) collective-permute-start(bf16[384,2048]{1,0:T(8,128)(2,1)S(1)} %get-tuple-element.179), channel_id=1, source_target_pairs={{0,16},{16,0},{32,48},{48,32},{64,80},{80,64},{96,112},{112,96},{1... | collective-permute-start | bytes 4718600 | tf_op jit(solution)/shard_map/ppermute | solution.py:41
  12.2 6.6 %collective-permute-start.15 = (f16[160,512]{1,0:T(8,128)(2,1)S(1)}, f16[160,512]{1,0:T(8,128)(2,1)S(1)}, u32[]{:S(2)}, u32[]{:S(2)}) collective-permute-start(f16[160,512]{1,0:T(8,128)(2,1)S(1)} %fusion.31), channel_id=1, source_target_pairs={{0,192},{16,208},{32,224},{48,240},{64,128},{80,144},{96,160},{112... | collective-permute-start | bytes 491528 | tf_op jit(solution)/shard_map/ppermute | solution.py:41
  13.9 5.5 %collective-permute-start.13 = (f16[176,512]{1,0:T(8,128)(2,1)S(1)}, f16[176,512]{1,0:T(8,128)(2,1)S(1)}, u32[]{:S(2)}, u32[]{:S(2)}) collective-permute-start(f16[176,512]{1,0:T(8,128)(2,1)S(1)} %get-tuple-element.212), channel_id=1, source_target_pairs={{0,64},{16,80},{32,96},{48,112},{64,0},{80,16},{96,32},{112,48},{1... | collective-permute-start | bytes 540680 | tf_op jit(solution)/shard_map/ppermute | solution.py:41
  14.0 5.5 %collective-permute-start.17 = (f16[176,512]{1,0:T(8,128)(2,1)S(1)}, f16[176,512]{1,0:T(8,128)(2,1)S(1)}, u32[]{:S(2)}, u32[]{:S(2)}) collective-permute-start(f16[176,512]{1,0:T(8,128)(2,1)S(1)} %get-tuple-element.213), channel_id=1, source_target_pairs={{0,32},{16,48},{32,0},{48,16},{64,96},{80,112},{96,64},{112,80},{1... | collective-permute-start | bytes 540680 | tf_op jit(solution)/shard_map/ppermute | solution.py:41
  18.9 15.3 %collective-permute-start.16 = (f16[160,512]{1,0:T(8,128)(2,1)S(1)}, f16[160,512]{1,0:T(8,128)(2,1)S(1)}, u32[]{:S(2)}, u32[]{:S(2)}) collective-permute-start(f16[160,512]{1,0:T(8,128)(2,1)S(1)} %fusion.21), channel_id=1, source_target_pairs={{0,32},{16,48},{32,0},{48,16},{64,96},{80,112},{96,64},{112,80},{1... | collective-permute-start | bytes 491528 | tf_op jit(solution)/shard_map/ppermute | solution.py:41
  19.7 15.5 %collective-permute-start.18 = (f16[176,512]{1,0:T(8,128)(2,1)S(1)}, f16[176,512]{1,0:T(8,128)(2,1)S(1)}, u32[]{:S(2)}, u32[]{:S(2)}) collective-permute-start(f16[176,512]{1,0:T(8,128)(2,1)S(1)} %get-tuple-element.208), channel_id=1, source_target_pairs={{0,64},{16,80},{32,96},{48,112},{64,0},{80,16},{96,32},{112,48},{1... | collective-permute-start | bytes 540680 | tf_op jit(solution)/shard_map/ppermute | solution.py:41
  20.9 7.2 %collective-permute-start.10 = (f16[2,160,512]{2,1,0:T(8,128)(2,1)S(1)}, f16[2,160,512]{2,1,0:T(8,128)(2,1)S(1)}, u32[]{:S(2)}, u32[]{:S(2)}) collective-permute-start(f16[2,160,512]{2,1,0:T(8,128)(2,1)S(1)} %multiply_convert_fusion.2), channel_id=1, source_target_pairs={{0,192},{16,208},{32,224},{48,240},{64,128},{80,144},{96,160},{112... | collective-permute-start | bytes 983048 | tf_op jit(solution)/shard_map/ppermute | solution.py:41
  22.8 9.9 %collective-permute-start.12 = (f16[2,176,512]{2,1,0:T(8,128)(2,1)S(1)}, f16[2,176,512]{2,1,0:T(8,128)(2,1)S(1)}, u32[]{:S(2)}, u32[]{:S(2)}) collective-permute-start(f16[2,176,512]{2,1,0:T(8,128)(2,1)S(1)} %get-tuple-element.210), channel_id=1, source_target_pairs={{0,64},{16,80},{32,96},{48,112},{64,0},{80,16},{96,32},{112,48},{1... | collective-permute-start | bytes 1081352 | tf_op jit(solution)/shard_map/ppermute | solution.py:41
  22.9 11.0 %collective-permute-start.11 = (f16[2,176,512]{2,1,0:T(8,128)(2,1)S(1)}, f16[2,176,512]{2,1,0:T(8,128)(2,1)S(1)}, u32[]{:S(2)}, u32[]{:S(2)}) collective-permute-start(f16[2,176,512]{2,1,0:T(8,128)(2,1)S(1)} %get-tuple-element.211), channel_id=1, source_target_pairs={{0,32},{16,48},{32,0},{48,16},{64,96},{80,112},{96,64},{112,80},{1... | collective-permute-start | bytes 1081352 | tf_op jit(solution)/shard_map/ppermute | solution.py:41
  28.1 7.8 %collective-permute-start.14 = (f16[176,512]{1,0:T(8,128)(2,1)S(1)}, f16[176,512]{1,0:T(8,128)(2,1)S(1)}, u32[]{:S(2)}, u32[]{:S(2)}) collective-permute-start(f16[176,512]{1,0:T(8,128)(2,1)S(1)} %get-tuple-element.209), channel_id=1, source_target_pairs={{0,192},{16,208},{32,224},{48,240},{64,128},{80,144},{96,160},{112... | collective-permute-start | bytes 540680 | tf_op jit(solution)/shard_map/ppermute | solution.py:41
  32.7 7.3 %collective-permute-start.25 = (f16[160,512]{1,0:T(8,128)(2,1)S(1)}, f16[160,512]{1,0:T(8,128)(2,1)S(1)}, u32[]{:S(2)}, u32[]{:S(2)}) collective-permute-start(f16[160,512]{1,0:T(8,128)(2,1)S(1)} %fusion.32), channel_id=1, source_target_pairs={{0,192},{16,208},{32,224},{48,240},{64,128},{80,144},{96,160},{112... | collective-permute-start | bytes 491528 | tf_op jit(solution)/shard_map/ppermute | solution.py:41
  34.0 7.7 %collective-permute-start.26 = (f16[160,512]{1,0:T(8,128)(2,1)S(1)}, f16[160,512]{1,0:T(8,128)(2,1)S(1)}, u32[]{:S(2)}, u32[]{:S(2)}) collective-permute-start(f16[160,512]{1,0:T(8,128)(2,1)S(1)} %fusion.30), channel_id=1, source_target_pairs={{0,32},{16,48},{32,0},{48,16},{64,96},{80,112},{96,64},{112,80},{1... | collective-permute-start | bytes 491528 | tf_op jit(solution)/shard_map/ppermute | solution.py:41
  34.1 8.9 %collective-permute-start.22 = (f16[176,512]{1,0:T(8,128)(2,1)S(1)}, f16[176,512]{1,0:T(8,128)(2,1)S(1)}, u32[]{:S(2)}, u32[]{:S(2)}) collective-permute-start(f16[176,512]{1,0:T(8,128)(2,1)S(1)} %get-tuple-element.206), channel_id=1, source_target_pairs={{0,64},{16,80},{32,96},{48,112},{64,0},{80,16},{96,32},{112,48},{1... | collective-permute-start | bytes 540680 | tf_op jit(solution)/shard_map/ppermute | solution.py:41
  35.1 8.0 %collective-permute-start.19 = (f16[176,512]{1,0:T(8,128)(2,1)S(1)}, f16[176,512]{1,0:T(8,128)(2,1)S(1)}, u32[]{:S(2)}, u32[]{:S(2)}) collective-permute-start(f16[176,512]{1,0:T(8,128)(2,1)S(1)} %get-tuple-element.207), channel_id=1, source_target_pairs={{0,32},{16,48},{32,0},{48,16},{64,96},{80,112},{96,64},{112,80},{1... | collective-permute-start | bytes 540680 | tf_op jit(solution)/shard_map/ppermute | solution.py:41
  35.9 5.9 %collective-permute-start.27 = (f16[160,512]{1,0:T(8,128)(2,1)S(1)}, f16[160,512]{1,0:T(8,128)(2,1)S(1)}, u32[]{:S(2)}, u32[]{:S(2)}) collective-permute-start(f16[160,512]{1,0:T(8,128)(2,1)S(1)} %fusion.23), channel_id=1, source_target_pairs={{0,64},{16,80},{32,96},{48,112},{64,0},{80,16},{96,32},{112,48},{1... | collective-permute-start | bytes 491528 | tf_op jit(solution)/shard_map/ppermute | solution.py:41
  40.0 5.8 %collective-permute-start.21 = (f16[176,512]{1,0:T(8,128)(2,1)S(1)}, f16[176,512]{1,0:T(8,128)(2,1)S(1)}, u32[]{:S(2)}, u32[]{:S(2)}) collective-permute-start(f16[176,512]{1,0:T(8,128)(2,1)S(1)} %get-tuple-element.202), channel_id=1, source_target_pairs={{0,192},{16,208},{32,224},{48,240},{64,128},{80,144},{96,160},{112... | collective-permute-start | bytes 540680 | tf_op jit(solution)/shard_map/ppermute | solution.py:41
  41.6 4.3 %collective-permute-start.24 = (f16[176,512]{1,0:T(8,128)(2,1)S(1)}, f16[176,512]{1,0:T(8,128)(2,1)S(1)}, u32[]{:S(2)}, u32[]{:S(2)}) collective-permute-start(f16[176,512]{1,0:T(8,128)(2,1)S(1)} %get-tuple-element.203), channel_id=1, source_target_pairs={{0,32},{16,48},{32,0},{48,16},{64,96},{80,112},{96,64},{112,80},{1... | collective-permute-start | bytes 540680 | tf_op jit(solution)/shard_map/ppermute | solution.py:41
  41.8 5.9 %collective-permute-start.23 = (f16[176,512]{1,0:T(8,128)(2,1)S(1)}, f16[176,512]{1,0:T(8,128)(2,1)S(1)}, u32[]{:S(2)}, u32[]{:S(2)}) collective-permute-start(f16[176,512]{1,0:T(8,128)(2,1)S(1)} %get-tuple-element.204), channel_id=1, source_target_pairs={{0,192},{16,208},{32,224},{48,240},{64,128},{80,144},{96,160},{112... | collective-permute-start | bytes 540680 | tf_op jit(solution)/shard_map/ppermute | solution.py:41
  43.0 4.7 %collective-permute-start.20 = (f16[176,512]{1,0:T(8,128)(2,1)S(1)}, f16[176,512]{1,0:T(8,128)(2,1)S(1)}, u32[]{:S(2)}, u32[]{:S(2)}) collective-permute-start(f16[176,512]{1,0:T(8,128)(2,1)S(1)} %get-tuple-element.205), channel_id=1, source_target_pairs={{0,64},{16,80},{32,96},{48,112},{64,0},{80,16},{96,32},{112,48},{1... | collective-permute-start | bytes 540680 | tf_op jit(solution)/shard_map/ppermute | solution.py:41
  64.4 17.7 %collective-permute-start.4 = (f16[176,512]{1,0:T(8,128)(2,1)S(1)}, f16[176,512]{1,0:T(8,128)(2,1)S(1)}, u32[]{:S(2)}, u32[]{:S(2)}) collective-permute-start(f16[176,512]{1,0:T(8,128)(2,1)S(1)} %get-tuple-element.126), channel_id=1, source_target_pairs={{0,4},{1,5},{2,6},{3,7},{4,0},{5,1},{6,2},{7,3},{8,12},{9,13},{10,... | collective-permute-start | bytes 540680 | tf_op jit(solution)/shard_map/cond/branch_2_fun/ppermute | solution.py:45
  68.4 21.0 %collective-permute-start.5 = (f16[336,512]{1,0:T(8,128)(2,1)S(1)}, f16[336,512]{1,0:T(8,128)(2,1)S(1)}, u32[]{:S(2)}, u32[]{:S(2)}) collective-permute-start(f16[336,512]{1,0:T(8,128)(2,1)S(1)} %convert_element_type.126), channel_id=1, source_target_pairs={{0,4},{1,5},{2,6},{3,7},{4,0},{5,1},{6,2},{7,3},{8,12},{9,13},{10,... | collective-permute-start | bytes 1032200 | tf_op jit(solution)/shard_map/cond/branch_2_fun/ppermute | solution.py:45
  89.6 1.0 %copy-start = (f32[1,512,512]{2,1,0:T(8,128)}, f32[1,512,512]{2,1,0:T(8,128)S(1)}, u32[]{:S(2)}) copy-start(f32[1,512,512]{2,1,0:T(8,128)S(1)} %get-tuple-element.171) | copy-start | bytes 3145732
